TPU v7x, 32 devices: a whole 2x2x4 slice. The times are simulated.
32 devices in a mesh: pool: 4 (over y, core), expert: 8 (over z, x).
Axes of the slice: x: 2, y: 2, z: 4, core: 2. Of those that a mesh axis runs over, the one named last changes fastest.
Arguments:
- residual: bfloat16 [64, 2, 4096], P('expert'), may hold values from -6 to 6
- queries: bfloat16 [64, 2, 32, 128], P('expert', None, 'pool'), may hold values from -150 to 150
- kv_cache: bfloat16 [64, 512, 2, 2, 128], P('expert'), may hold values from -6 to 6
- kv_pages: bfloat16 [16, 8, 64, 2, 2, 128], P('pool', 'expert'), may hold values from -6 to 6
- cache_len: int32 [64], P('expert'), may hold values from 1 to 510, 16320 in all
- page_row: int32 [16, 8], P(None, 'expert'), may hold values from 0 to 7
- page_len: int32 [16, 8], P(None, 'expert'), may hold values from 1 to 64
- routes: int32 [64, 2, 8], P('expert'), may hold values from 0 to 15, all different within a row; in each aligned block of 16 rows (0 to 15, 16 to 31, ..., all dimensions but the last counted through in order) at most 12 rows name the same one
- route_weight: float32 [64, 2, 8], P('expert'), may hold values from 0.05 to 0.5
- out_weight: bfloat16 [4096, 4096], P('pool'), may hold values from -1.5 to 1.5
- gate_weight: bfloat16 [16, 4096, 1024], P('expert', None, 'pool'), may hold values from -0.09375 to 0.09375
- up_weight: bfloat16 [16, 4096, 1024], P('expert', None, 'pool'), may hold values from -0.09375 to 0.09375
- down_weight: bfloat16 [16, 1024, 4096], P('expert', 'pool'), may hold values from -0.375 to 0.375
Outputs:
- layer_out: bfloat16 [64, 2, 4096], P('expert')
Inputs may be any that keep to these rules, and one draw needn't show every extreme that they name: The row's two new tokens sit at positions cache_len and cache_len + 1 of its cache. The page belongs to row e * 8 + page_row of its group e. `routes`: a token names distinct experts; among the 16 new tokens of one device's rows no expert is named by more than 12 tokens.
All inputs are finite; a program needn't handle non-finite values. No bound on the sum of `cache_len` on one device may be relied on, other than what follows from the above.
Results may differ from a plain program's by a relative error of at most 0.028.
Values may be sent and summed in bfloat16 or wider, within the bound.
No kernel may reach another device: no remote copies, remote signals or barrier semaphores. Data moves between devices by JAX's collectives and lax.ppermute only.
A program may use at most 64 MiB of HBM per device.

v0:
```python
import math

import jax
import jax.numpy as jnp
import numpy as np
from jax import lax
from jax.sharding import PartitionSpec as P

very_low = -1e30


def masked_top(scores, allowed):
    return jnp.max(jnp.where(allowed, scores, very_low), axis=-1)


def spread_weights(scores, allowed, row_top):
    return jnp.where(allowed, jnp.exp(scores - row_top[..., None]), 0.0)


def per_device(
    residual,
    queries,
    kv_cache,
    kv_pages,
    cache_len,
    page_row,
    page_len,
    routes,
    route_weight,
    out_weight,
    gate_weight,
    up_weight,
    down_weight,
):
    pool_size = lax.axis_size("pool")
    expert_size = lax.axis_size("expert")
    pool_index = lax.axis_index("pool")
    rows_here, step_count, heads_here, head_dim = queries.shape
    kv_heads = kv_cache.shape[2]
    page_size = kv_pages.shape[2]
    model_width = residual.shape[2]
    score_scale = 1.0 / math.sqrt(head_dim)
    group_head = pool_index * kv_heads // pool_size
    own_cache = lax.dynamic_index_in_dim(kv_cache, group_head, 2, keepdims=False)
    cache_keys = own_cache[:, :, 0]
    cache_values = own_cache[:, :, 1]
    last_seen = cache_len[:, None] + jnp.arange(step_count, dtype=jnp.int32)[None, :]
    cache_valid = (
        jnp.arange(kv_cache.shape[1], dtype=jnp.int32)[None, None, :] <= last_seen[:, :, None]
    )[:, :, None, :]
    cache_scores = (
        jnp.einsum("rthd,rld->rthl", queries, cache_keys, preferred_element_type=jnp.float32)
        * score_scale
    )
    row_ids = jnp.arange(rows_here, dtype=jnp.int32)
    token_ids = jnp.arange(page_size, dtype=jnp.int32)
    owner_rows = page_row[:, 0]
    owner_sizes = page_len[:, 0]
    dest_heads = np.arange(pool_size) * kv_heads // pool_size
    outgoing = jnp.take(kv_pages[:, 0], dest_heads, axis=2)
    arrived = lax.all_to_all(outgoing, "pool", split_axis=2, concat_axis=0, tiled=True)
    page_keys = arrived[:, :, 0, 0].reshape(-1, head_dim)
    page_values = arrived[:, :, 0, 1].reshape(-1, head_dim)
    page_valid = (owner_rows[None, :, None] == row_ids[:, None, None]) & (
        token_ids[None, :] < owner_sizes[:, None]
    )[None]
    page_valid = page_valid.reshape(rows_here, 1, 1, -1)
    page_scores = (
        jnp.einsum("rthd,kd->rthk", queries, page_keys, preferred_element_type=jnp.float32)
        * score_scale
    )
    row_top = jnp.maximum(
        masked_top(cache_scores, cache_valid), masked_top(page_scores, page_valid)
    )
    cache_weights = spread_weights(cache_scores, cache_valid, row_top)
    page_weights = spread_weights(page_scores, page_valid, row_top)
    row_total = jnp.sum(cache_weights, axis=-1) + jnp.sum(page_weights, axis=-1)
    mixed_sum = jnp.einsum(
        "rthl,rld->rthd",
        cache_weights.astype(jnp.bfloat16),
        cache_values,
        preferred_element_type=jnp.float32,
    )
    mixed_sum = mixed_sum + jnp.einsum(
        "rthk,kd->rthd",
        page_weights.astype(jnp.bfloat16),
        page_values,
        preferred_element_type=jnp.float32,
    )
    attended = mixed_sum / row_total[..., None]
    tokens_here = rows_here * step_count
    attended_low = attended.astype(jnp.bfloat16).reshape(tokens_here, heads_here * head_dim)
    projected = jnp.dot(attended_low, out_weight, preferred_element_type=jnp.float32)
    projected = lax.psum(projected.astype(jnp.bfloat16), "pool").astype(jnp.float32)
    hidden = residual.reshape(tokens_here, model_width).astype(jnp.float32) + projected
    hidden_low = hidden.astype(jnp.bfloat16)
    local_experts = gate_weight.shape[0]
    experts = local_experts * expert_size
    top_count = routes.shape[2]
    capacity = max(2, (3 * rows_here * top_count + experts - 1) // experts)
    flat_routes = routes.reshape(tokens_here * top_count)
    pick_table = (flat_routes[:, None] == jnp.arange(experts, dtype=jnp.int32)[None, :]).astype(
        jnp.int32
    )
    slot_index = jnp.sum((jnp.cumsum(pick_table, axis=0) - 1) * pick_table, axis=1)
    position = flat_routes * capacity + slot_index
    token_position = position.reshape(tokens_here, top_count)
    slot_ids = jnp.arange(experts * capacity, dtype=jnp.int32)
    select_tokens = jnp.sum(
        (token_position[:, :, None] == slot_ids[None, None, :]).astype(jnp.int32), axis=1
    ).astype(jnp.bfloat16)
    column_count = model_width // pool_size
    outgoing_rows = jnp.einsum(
        "tc,td->cd", select_tokens, hidden_low, preferred_element_type=jnp.float32
    ).astype(jnp.bfloat16)
    arrived_rows = lax.all_to_all(outgoing_rows, "expert", split_axis=0, concat_axis=0, tiled=True)
    batched = arrived_rows.reshape(expert_size, local_experts, capacity, model_width)
    gate_value = jnp.einsum(
        "sjcd,jdf->sjcf", batched, gate_weight, preferred_element_type=jnp.float32
    )
    upward = jnp.einsum("sjcd,jdf->sjcf", batched, up_weight, preferred_element_type=jnp.float32)
    active = (jax.nn.silu(gate_value) * upward).astype(jnp.bfloat16)
    partial_value = jnp.einsum(
        "sjcf,jfd->sjcd", active, down_weight, preferred_element_type=jnp.float32
    ).astype(jnp.bfloat16)
    partial_value = partial_value.reshape(experts * capacity, model_width)
    pair_weights = route_weight.reshape(tokens_here, top_count)
    shares = lax.psum_scatter(
        partial_value.astype(jnp.float32).astype(jnp.bfloat16),
        "pool",
        scatter_dimension=1,
        tiled=True,
    ).astype(jnp.float32)
    returned = lax.all_to_all(
        shares.astype(jnp.bfloat16), "expert", split_axis=0, concat_axis=0, tiled=True
    ).astype(shares.dtype)
    picked = jnp.take(returned, position, axis=0).reshape(tokens_here, top_count, column_count)
    weighted = jnp.sum(pair_weights[..., None] * picked, axis=1)
    expert_sum = lax.all_gather(weighted.astype(jnp.bfloat16), "pool", axis=1, tiled=True).astype(
        weighted.dtype
    )
    output = (hidden + expert_sum).astype(jnp.bfloat16).reshape(rows_here, step_count, model_width)
    return output


def solution(mesh):
    return jax.shard_map(
        per_device,
        mesh=mesh,
        in_specs=(
            P("expert", None, None),
            P("expert", None, "pool", None),
            P("expert", None, None, None, None),
            P("pool", "expert", None, None, None, None),
            P("expert"),
            P(None, "expert"),
            P(None, "expert"),
            P("expert", None, None),
            P("expert", None, None),
            P("pool", None),
            P("expert", None, "pool"),
            P("expert", None, "pool"),
            P("expert", "pool", None),
        ),
        out_specs=P("expert", None, None),
        check_vma=False,
    )
```

profile of v0, /device:TPU:0, one launch (start us, length us, event | category | flops | bytes accessed | tf_op | source)
XLA Modules:
  0.0 172.4 jit_solution(2310746984805556101)
XLA Ops:
  6.5 0.7 pad_clamp_fusion.1
  7.2 0.3 copy-done
  7.5 2.7 %gather_fusion = bf16[4,4,64,2,128]{4,3,2,1,0:T(2,128)(2,1)} fusion(bf16[4,64,2,2,128]{4,3,2,1,0:T(2,128)(2,1)S(1)} %bitcast.105, s32[1024]{0:T(1024)S(1)} %pad_clamp_fusion.1), kind=kCustom, calls=%fused_computation | custom fusion | bytes 1048592 | tf_op jit(solution)/shard_map/jit(_take)/gather | solution.py:60
  10.2 4.3 %all-to-all-start = ((bf16[4,64,4,2,128]{4,3,1,0,2:T(2,128)(2,1)}), bf16[4,64,4,2,128]{4,3,1,0,2:T(2,128)(2,1)S(1)}, u32[]{:S(2)}, u32[]{:S(2)}) async-start(bf16[4,64,4,2,128]{4,3,1,0,2:T(2,128)(2,1)} %bitcast.8), calls=%async_computation | async-start | bytes 1048576 | tf_op jit(solution)/shard_map/all_to_all | solution.py:61
  14.4 0.0 all-reduce.2.cloned.1.call-start
  14.5 0.1 reshape.181
  14.6 3.0 %constant_dynamic-slice_fusion = bf16[8,512,1,2,128]{4,3,2,1,0:T(2,128)(2,1)S(1)} fusion(bf16[8,512,2,2,128]{4,3,2,1,0:T(2,128)(2,1)} %param.16, s32[]{:T(128)S(6)} %select_n.55), kind=kLoop, calls=%fused_computation.69 | loop fusion | bytes 4194308 | tf_op jit(solution)/shard_map/jit(dynamic_index_in_dim)/dynamic_slice | solution.py:44
  17.6 0.0 copy-start.9
  17.6 0.0 copy-start.11
  17.6 0.0 copy-start.10
  17.6 0.0 copy-start.5
  17.6 0.0 copy-start.6
  17.7 0.4 copy.53
  18.1 0.2 copy-done.9
  18.3 0.1 iota_add_fusion
  18.3 0.1 iota_compare_fusion.2
  18.4 0.1 and.39
  18.5 0.1 and.40
  18.6 0.1 lt.53
  18.7 0.0 copy-done.10
  18.7 0.1 broadcast_reduce_fusion
  18.8 0.1 lt.55
  18.9 0.1 fusion.40
  19.0 0.2 reduce_window_sum.11
  19.2 0.2 select_reduce_fusion.2
  19.3 0.1 reduce_sum.52
  19.4 0.0 copy-done.5
  19.5 0.0 copy-done.6
  19.5 0.5 select_reduce_fusion.1
  20.0 3.3 %all-to-all-done = bf16[4,64,4,2,128]{4,3,1,0,2:T(2,128)(2,1)S(1)} async-done(((bf16[4,64,4,2,128]{4,3,1,0,2:T(2,128)(2,1)}), bf16[4,64,4,2,128]{4,3,1,0,2:T(2,128)(2,1)S(1)}, u32[]{:S(2)}, u32[]{:S(2)}) %all-to-all-start) | async-done | bytes 524320 | tf_op jit(solution)/shard_map/all_to_all | solution.py:61
  23.3 1.1 fusion.47
  24.4 0.3 select_reduce_fusion
  24.8 0.3 fusion.24
  25.0 0.2 fusion.31
  25.3 0.3 fusion.26
  25.6 0.3 fusion.21
  25.9 5.3 %convolution_convert_fusion.2 = bf16[16,4096]{1,0:T(8,128)(2,1)} fusion(bf16[1024,4096]{1,0:T(8,128)(2,1)} %param.23, bf16[2,8,8,128]{3,2,1,0:T(8,128)(2,1)S(1)} %bitcast.115), kind=kOutput, calls=%fused_computation.5 | convolution fusion | flops 134283264 | bytes 8552448 | tf_op jit(solution)/shard_map/dot_general | solution.py:93
  31.2 0.0 all-reduce.2.cloned.1.call-update
  31.2 0.0 reduce-scatter.2.cloned.1.call-start
  31.2 0.1 convert_reduce_fusion
  31.3 32.7 %all-reduce.2.cloned.1.call-done = bf16[16,4096]{1,0:T(8,128)(2,1)} async-done(((bf16[16,4096]{1,0:T(8,128)(2,1)}), bf16[16,4096]{1,0:T(8,128)(2,1)}) %all-reduce.2.cloned.1.call-update) | async-done | bytes 131088 | tf_op jit(solution)/shard_map/psum | solution.py:94
  64.1 1.5 convolution_convert_fusion.1
  65.6 0.0 copy-start.1
  65.6 41.5 %all_to_all.36 = bf16[8,24,4096]{2,1,0:T(8,128)(2,1)S(1)} all-to-all(bf16[8,24,4096]{2,1,0:T(8,128)(2,1)S(1)} %bitcast.108), channel_id=1, replica_groups=mesh['pool'=4,'expert'=8] {'expert'}, dimensions={0} | all-to-all | bytes 3145728 | tf_op jit(solution)/shard_map/all_to_all | solution.py:116
  107.1 0.9 copy.33
  108.0 0.0 copy-start.2
  108.0 0.8 fusion.8
  108.8 1.4 copy-done.2
  110.2 0.8 fusion.17
  111.0 1.4 copy-done.3
  112.4 0.7 fusion
  113.1 0.1 copy.35
  113.2 1.4 reshape.183
  114.6 0.0 reduce-scatter.2.cloned.1.call-update
  114.6 26.5 %reduce-scatter.2.cloned.1.call-done = bf16[192,1024]{1,0:T(8,128)(2,1)} async-done(((bf16[192,4096]{1,0:T(8,128)(2,1)}), bf16[192,1024]{1,0:T(8,128)(2,1)}) %reduce-scatter.2.cloned.1.call-update) | async-done | bytes 393232 | tf_op jit(solution)/shard_map/reduce_scatter | solution.py:128
  141.1 5.5 %all-to-all-start.2 = ((bf16[8,24,1024]{2,1,0:T(8,128)(2,1)}), bf16[8,24,1024]{2,1,0:T(8,128)(2,1)S(1)}, u32[]{:S(2)}, u32[]{:S(2)}) async-start(bf16[8,24,1024]{2,1,0:T(8,128)(2,1)} %bitcast.114), calls=%async_computation.3 | async-start | bytes 786432 | tf_op jit(solution)/shard_map/all_to_all | solution.py:134
  146.6 0.1 mul.82
  146.7 11.4 %all-to-all-done.2 = bf16[8,24,1024]{2,1,0:T(8,128)(2,1)S(1)} async-done(((bf16[8,24,1024]{2,1,0:T(8,128)(2,1)}), bf16[8,24,1024]{2,1,0:T(8,128)(2,1)S(1)}, u32[]{:S(2)}, u32[]{:S(2)}) %all-to-all-start.2) | async-done | bytes 393248 | tf_op jit(solution)/shard_map/all_to_all | solution.py:134
  158.2 0.1 bitcast_convert_fusion
  158.3 0.0 copy-start.8
  158.3 0.8 gather_fusion.1
  159.1 0.3 fusion.23
  159.4 5.4 %all_gather.3 = bf16[16,4096]{1,0:T(8,128)(2,1)S(1)} all-gather(bf16[16,1024]{1,0:T(8,128)(2,1)S(1)} %fusion.23), channel_id=1, replica_groups=mesh['pool'=4,'expert'=8] {'pool'}, dimensions={1}, use_global_device_ids=true | all-gather | bytes 163840 | tf_op jit(solution)/shard_map/all_gather | solution.py:139
  164.8 0.8 reshape.184
  (23 shorter events, 0.3 us)
Async XLA Ops:
  6.5 1.0 copy-start
  6.5 7.9 %copy-start.7 = (s32[8,2,8]{2,1,0:T(2,128)S(1)}, s32[8,2,8]{2,1,0:T(2,128)}, u32[]{:S(2)}) copy-start(s32[8,2,8]{2,1,0:T(2,128)} %param.21) | copy-start | bytes 1540
  10.2 13.1 %all-to-all-start = ((bf16[4,64,4,2,128]{4,3,1,0,2:T(2,128)(2,1)}), bf16[4,64,4,2,128]{4,3,1,0,2:T(2,128)(2,1)S(1)}, u32[]{:S(2)}, u32[]{:S(2)}) async-start(bf16[4,64,4,2,128]{4,3,1,0,2:T(2,128)(2,1)} %bitcast.8), calls=%async_computation | async-start | bytes 1048576 | tf_op jit(solution)/shard_map/all_to_all | solution.py:61
  14.4 49.6 %all-reduce.2.cloned.1.call-start = ((), (), s32[]{:S(2)}) async-start(), calls=%async_computation.4 | async-start | bytes 262144 | tf_op jit(solution)/shard_map/psum | solution.py:94
  17.6 0.7 copy-start.9
  17.6 0.8 copy-start.11
  17.6 1.1 copy-start.10
  17.6 1.8 %copy-start.5 = (bf16[8,2,4096]{2,1,0:T(2,128)(2,1)S(1)}, bf16[8,2,4096]{2,1,0:T(2,128)(2,1)}, u32[]{:S(2)}) copy-start(bf16[8,2,4096]{2,1,0:T(2,128)(2,1)} %param.14) | copy-start | bytes 393220
  17.6 1.9 %copy-start.6 = (bf16[8,2,8,128]{3,2,1,0:T(8,128)(2,1)S(1)}, bf16[8,2,8,128]{3,2,1,0:T(8,128)(2,1)}, u32[]{:S(2)}) copy-start(bf16[8,2,8,128]{3,2,1,0:T(8,128)(2,1)} %param.15) | copy-start | bytes 98308
  31.2 109.9 %reduce-scatter.2.cloned.1.call-start = ((), (), s32[]{:S(2)}) async-start(), calls=%async_computation.5 | async-start | bytes 1966080 | tf_op jit(solution)/shard_map/reduce_scatter | solution.py:128
  65.6 42.4 %copy-start.1 = (bf16[2,4096,256]{2,1,0:T(8,128)(2,1)S(1)}, bf16[2,4096,256]{2,1,0:T(8,128)(2,1)}, u32[]{:S(2)}) copy-start(bf16[2,4096,256]{2,1,0:T(8,128)(2,1)} %param.24) | copy-start | bytes 12582916
  108.0 2.2 %copy-start.2 = (bf16[2,4096,256]{2,1,0:T(8,128)(2,1)S(1)}, bf16[2,4096,256]{2,1,0:T(8,128)(2,1)}, u32[]{:S(2)}) copy-start(bf16[2,4096,256]{2,1,0:T(8,128)(2,1)} %param.25) | copy-start | bytes 12582916
  110.2 2.2 %copy-start.3 = (bf16[2,256,4096]{2,1,0:T(8,128)(2,1)S(1)}, bf16[2,256,4096]{2,1,0:T(8,128)(2,1)}, u32[]{:S(2)}) copy-start(bf16[2,256,4096]{2,1,0:T(8,128)(2,1)} %param.26) | copy-start | bytes 12582916
  141.1 17.0 %all-to-all-start.2 = ((bf16[8,24,1024]{2,1,0:T(8,128)(2,1)}), bf16[8,24,1024]{2,1,0:T(8,128)(2,1)S(1)}, u32[]{:S(2)}, u32[]{:S(2)}) async-start(bf16[8,24,1024]{2,1,0:T(8,128)(2,1)} %bitcast.114), calls=%async_computation.3 | async-start | bytes 786432 | tf_op jit(solution)/shard_map/all_to_all | solution.py:134
  158.3 0.8 copy-start.8
  158.3 6.5 %copy-start.4 = (bf16[16,4096]{1,0:T(8,128)(2,1)S(1)}, bf16[16,4096]{1,0:T(8,128)(2,1)}, u32[]{:S(2)}) copy-start(bf16[16,4096]{1,0:T(8,128)(2,1)} %all-reduce.2.cloned.1.call-done) | copy-start | bytes 393220
Sparse Core Ops, SparseCore 0:
  31.3 32.7 all-reduce.1
  114.7 26.3 reduce-scatter.1
where the time goes:
time: 173 us; the launch traced here: 172 us
  waiting for transfers between devices  73.9 us (43%)
  blocking collectives  47 us (27%)
  local copies, waits for them, and re-layouts  15.2 us (9%)
  between operations  13.7 us (8%)
  matrix products  10.4 us (6%)
  starting transfers between devices  9.81 us (6%)
  other arithmetic  2.34 us (1%)
    all_to_all x1, blocking collectives, per_device(): lax.all_to_all(outgoing_rows, 'expert', split_axis=0, concat_axis=0, tile...  41.5 us
    psum x1, waiting for transfers between devices, per_device(): lax.psum(projected.astype(jnp.bfloat16), 'pool').astype(jnp.float32)  32.7 us
    reduce_scatter x1, waiting for transfers between devices, per_device(): lax.psum_scatter(partial_value.astype(jnp.float32).astype(jnp.bfloat16),...  26.5 us
    all_to_all x1, waiting for transfers between devices, per_device(): lax.all_to_all(shares.astype(jnp.bfloat16), 'expert', split_axis=0, conca...  11.4 us
    all_to_all x1, starting transfers between devices, per_device(): lax.all_to_all(shares.astype(jnp.bfloat16), 'expert', split_axis=0, conca...  5.5 us
    all_gather x1, blocking collectives, per_device(): lax.all_gather(weighted.astype(jnp.bfloat16), 'pool', axis=1, tiled=True)  5.42 us
    dot_general x1, matrix products, per_device(): jnp.dot(attended_low, out_weight, preferred_element_type=jnp.float32)  5.25 us
    all_to_all x1, starting transfers between devices, per_device(): lax.all_to_all(outgoing, 'pool', split_axis=2, concat_axis=0, tiled=True)  4.26 us
  transfers between devices with their start and end apart: 4, of which 4 were waited for; matrix products, arithmetic and copies ran while one was open for 3% of the time, Pallas kernels for 0%

commit v1 on v0

v1 whole, which is shorter than its diff:
```python
import functools
import math

import jax
import jax.numpy as jnp
from jax import lax
from jax.experimental import pallas as pl
from jax.experimental.pallas import tpu as pltpu
from jax.sharding import PartitionSpec as P

MIB = 1 << 20
LANES = 128
very_low = -1e30
VMEM = pl.BlockSpec(memory_space=pltpu.VMEM)
SMEM = pl.BlockSpec(memory_space=pltpu.SMEM)
float32 = jnp.float32
bfloat16 = jnp.bfloat16


def dot_t(a, b):
    return lax.dot_general(a, b, (((1,), (1,)), ((), ())), preferred_element_type=float32)


def dot(a, b):
    return jnp.dot(a, b, preferred_element_type=float32)


def cache_kernel(heads, kv_heads, scale, head_ref, len_ref, q_ref, kv_ref, acc_ref, top_ref, total_ref):
    row = pl.program_id(0)
    kv = kv_ref[0]
    scores = dot_t(q_ref[0], kv) * scale
    lane = lax.broadcasted_iota(jnp.int32, scores.shape, 1)
    token = lax.broadcasted_iota(jnp.int32, scores.shape, 0) // heads
    wide = 2 * kv_heads
    seen = (lane // wide <= len_ref[row] + token) & (lane % wide == 2 * head_ref[0])
    scores = jnp.where(seen, scores, very_low)
    top = jnp.max(scores, axis=1, keepdims=True)
    weights = jnp.where(seen, jnp.exp(scores - top), 0.0)
    total = jnp.sum(weights, axis=1, keepdims=True)
    shifted = pltpu.roll(weights, 1, 1).astype(bfloat16)
    acc_ref[0] = dot(shifted, kv)
    top_ref[0] = jnp.broadcast_to(top, top_ref.shape[1:])
    total_ref[0] = jnp.broadcast_to(total, total_ref.shape[1:])


def page_kernel(
    heads, steps, page_size, scale, count, info_ref, page_row_ref, page_len_ref, q_ref, acc_ref, top_ref, total_ref, *rest
):
    pages = rest[:count]
    weight_ref, low_ref, send_ref, flat_ref = rest[count:]
    q = q_ref[...]
    rows = q.shape[0]
    span = 2 * page_size
    parts, allowed = [], []
    owner = lax.broadcasted_iota(jnp.int32, (rows, span), 0) // (heads * steps)
    lane = lax.broadcasted_iota(jnp.int32, (rows, span), 1)
    keys = jnp.where(lane % 2 == 0, lane // 2, page_size)
    for n in range(count):
        part = dot_t(q, pages[n][...]) * scale
        here = part.shape[1] // span
        for i in range(here):
            page = info_ref[1 + n] * here + i
            ok = (owner == page_row_ref[page, 0]) & (keys < page_len_ref[page, 0])
            allowed.append(ok)
            parts.append(jnp.where(ok, part[:, i * span : (i + 1) * span], very_low))
    scores = jnp.concatenate(parts, axis=1)
    seen = jnp.concatenate(allowed, axis=1)
    cache_top = top_ref[...]
    page_top = jnp.max(scores, axis=1, keepdims=True)
    top = jnp.maximum(cache_top, page_top)
    weights = jnp.where(seen, jnp.exp(scores - top[:, :1]), 0.0)
    shrink = jnp.exp(cache_top - top)
    total = total_ref[...] * shrink + jnp.sum(weights, axis=1, keepdims=True)
    shifted = pltpu.roll(weights, 1, 1).astype(bfloat16)
    mixed = acc_ref[...] * shrink
    size = shifted.shape[1] // count
    for n in range(count):
        mixed = mixed + dot(shifted[:, n * size : (n + 1) * size], pages[n][...])
    flat_ref[...] = mixed / total
    tokens = rows // heads
    low = jnp.concatenate(
        [flat_ref[pl.ds(h, tokens, stride=heads), :].astype(bfloat16) for h in range(heads)], axis=1
    )
    low_ref[...] = low
    half = send_ref.shape[1]
    start = pl.multiple_of((1 - info_ref[0]) * half, half)
    send_ref[...] = dot(low, weight_ref[:, pl.ds(start, half)]).astype(bfloat16)


def project_kernel(core_ref, low_ref, weight_ref, keep_ref):
    half = keep_ref.shape[1]
    start = pl.multiple_of(core_ref[0] * half, half)
    keep_ref[...] = dot(low_ref[...], weight_ref[:, pl.ds(start, half)])


def expert_kernel(count, info_ref, *rest):
    own, other = rest[:count], rest[count : 2 * count]
    gate_ref, up_ref, down_ref, act_ref, send_ref = rest[2 * count :]
    half = send_ref.shape[1]
    own_all = jnp.concatenate([r[...] for r in own], axis=0)
    other_all = jnp.concatenate([r[:, :half] for r in other], axis=0)
    table = own_all[:, half:].astype(float32)
    own_all = own_all[:, :half]
    lane = lax.broadcasted_iota(jnp.int32, table.shape, 1)
    core = info_ref[0]
    first = pl.ds(pl.multiple_of(core * half, half), half)
    second = pl.ds(pl.multiple_of((1 - core) * half, half), half)
    experts, _, units = gate_ref.shape
    everyone = info_ref[2]
    for j in range(experts):
        mine = info_ref[1] * experts + j
        weight = jnp.sum(
            jnp.where((lane == mine) | (lane == mine + everyone), table, 0.0), axis=1, keepdims=True
        )
        gate = dot(own_all, gate_ref[j, first, :]) + dot(other_all, gate_ref[j, second, :])
        up = dot(own_all, up_ref[j, first, :]) + dot(other_all, up_ref[j, second, :])
        active = gate / (1.0 + jnp.exp(-gate)) * up
        act_ref[:, j * units : (j + 1) * units] = (active * weight).astype(bfloat16)
    total = 0.0
    for j in range(experts):
        total = total + dot(act_ref[:, j * units : (j + 1) * units], down_ref[j, :, second])
    send_ref[...] = total.astype(bfloat16)


def down_kernel(info_ref, act_ref, down_ref, keep_ref):
    half = keep_ref.shape[1]
    experts, units, _ = down_ref.shape
    first = pl.ds(pl.multiple_of(info_ref[0] * half, half), half)
    total = 0.0
    for j in range(experts):
        total = total + dot(act_ref[:, j * units : (j + 1) * units], down_ref[j, :, first])
    keep_ref[...] = total.astype(bfloat16)


def call(kernel, outs, specs, scratch=(), vmem=16, flops=0, bytes_accessed=0, **kw):
    return pl.pallas_call(
        kernel,
        out_shape=outs,
        in_specs=specs,
        out_specs=jax.tree.map(lambda _: VMEM, outs),
        scratch_shapes=scratch,
        compiler_params=pltpu.CompilerParams(vmem_limit_bytes=vmem * MIB),
        cost_estimate=pl.CostEstimate(flops=flops, bytes_accessed=bytes_accessed, transcendentals=0),
        **kw,
    )


def per_device(
    residual,
    queries,
    kv_cache,
    kv_pages,
    cache_len,
    page_row,
    page_len,
    routes,
    route_weight,
    out_weight,
    gate_weight,
    up_weight,
    down_weight,
):
    pool_size = lax.axis_size("pool")
    expert_size = lax.axis_size("expert")
    pool_index = lax.axis_index("pool")
    expert_index = lax.axis_index("expert")
    cores, near = 2, 2
    outer, far = pool_size // cores, expert_size // near
    core = pool_index % cores

    def swap(value, pool_flip=0, expert_flip=0):
        pairs = []
        for p in range(pool_size):
            for e in range(expert_size):
                pairs.append((p * expert_size + e, (p ^ pool_flip) * expert_size + (e ^ expert_flip)))
        return lax.ppermute(value, ("pool", "expert"), pairs)

    rows, steps, heads, head_dim = queries.shape
    length, kv_heads = kv_cache.shape[1:3]
    held, _, page_size = kv_pages.shape[:3]
    width = residual.shape[2]
    half = width // cores
    tokens = rows * steps
    scale = 1.0 / math.sqrt(head_dim)

    def head_of(pool):
        return pool * kv_heads // pool_size

    def pages_for(pool):
        picked = lax.dynamic_index_in_dim(kv_pages[:, 0], head_of(pool), 2, keepdims=False)
        return picked.reshape(held * page_size * 2, head_dim)

    my_head = head_of(pool_index)
    own_pages = pages_for(pool_index)
    sets, sources = [own_pages], [pool_index]
    for k in range(1, outer):
        flip = k * cores
        sets.append(swap(pages_for(pool_index ^ flip), flip))
        sources.append(pool_index ^ flip)
    for n in range(outer):
        sets.append(swap(sets[n], 1))
        sources.append(sources[n] ^ 1)

    group = steps * heads
    q_rows = queries.reshape(rows, group, head_dim)
    deep = length * kv_heads * 2
    kv_rows = kv_cache.reshape(rows, deep, head_dim)
    stat = jax.ShapeDtypeStruct((rows, group, head_dim), float32)
    block = lambda n: pl.BlockSpec((1, n, head_dim), lambda r: (r, 0, 0))
    acc, top, total = pl.pallas_call(
        functools.partial(cache_kernel, heads, kv_heads, scale),
        out_shape=(stat, stat, stat),
        grid=(rows,),
        in_specs=[SMEM, SMEM, block(group), block(deep)],
        out_specs=(block(group),) * 3,
        compiler_params=pltpu.CompilerParams(vmem_limit_bytes=8 * MIB),
        cost_estimate=pl.CostEstimate(
            flops=4 * rows * group * deep * head_dim, bytes_accessed=kv_cache.size * 2, transcendentals=rows * group * deep
        ),
    )(my_head[None], cache_len, q_rows, kv_rows)

    flat = lambda a: a.reshape(rows * group, head_dim)
    info = jnp.stack([core] + sources)
    low, send = call(
        functools.partial(page_kernel, heads, steps, page_size, scale, pool_size),
        (
            jax.ShapeDtypeStruct((tokens, heads * head_dim), bfloat16),
            jax.ShapeDtypeStruct((tokens, half), bfloat16),
        ),
        [SMEM] * 3 + [VMEM] * (4 + pool_size + 1),
        scratch=[pltpu.VMEM((rows * group, head_dim), float32)],
        flops=2 * tokens * heads * head_dim * half,
    )(info, page_row, page_len, flat(q_rows), flat(acc), flat(top), flat(total), *sets, out_weight)
    arrived = swap(send, 1)
    keep = call(
        project_kernel, jax.ShapeDtypeStruct((tokens, half), float32), [SMEM, VMEM, VMEM],
        flops=2 * tokens * heads * head_dim * half,
    )(core[None], low, out_weight)

    experts = gate_weight.shape[0] * expert_size
    wide = -(-2 * experts // LANES) * LANES
    routes = routes.reshape(tokens, -1)
    named = routes[:, :, None] == jnp.arange(wide, dtype=jnp.int32) % experts
    table = jnp.sum(jnp.where(named, route_weight.reshape(tokens, -1, 1), 0.0), axis=1)
    coarse = lax.reduce_precision(table, 8, 7)
    table = jnp.where(jnp.arange(wide) < experts, coarse, jnp.where(jnp.arange(wide) < 2 * experts, table - coarse, 0.0))

    own_residual = lax.dynamic_slice_in_dim(residual.reshape(tokens, width), core * half, half, 1).astype(float32)
    first = pool_index // cores == 0
    partial = keep + arrived.astype(float32) + jnp.where(first, own_residual, 0.0)
    message = jnp.concatenate([partial, table], axis=1).astype(bfloat16)

    got = {(0, 0): message}
    for e in range(near):
        for k in range(outer):
            if k or e:
                got[k, e] = swap(message, k * cores, e)
    hiddens = []
    for e in range(near):
        total = got[0, e][:, :half].astype(float32)
        for k in range(1, outer):
            total = total + got[k, e][:, :half].astype(float32)
        hiddens.append(total)
    block_low = jnp.concatenate(
        [jnp.concatenate([hiddens[e].astype(bfloat16), got[0, e][:, half:]], axis=1) for e in range(near)], axis=0
    )
    blocks = [block_low] + [swap(block_low, 0, k * near) for k in range(1, far)]
    others = [swap(b, 1) for b in blocks]

    everyone = tokens * near * far
    units = gate_weight.shape[0] * gate_weight.shape[2]
    expert_info = jnp.stack([core, expert_index, jnp.int32(experts)])
    act, outgoing = call(
        functools.partial(expert_kernel, far),
        (
            jax.ShapeDtypeStruct((everyone, units), bfloat16),
            jax.ShapeDtypeStruct((everyone, half), bfloat16),
        ),
        [SMEM] + [VMEM] * (2 * far + 3),
        vmem=24,
        flops=4 * everyone * width * units,
    )(expert_info, *blocks, *others, gate_weight, up_weight, down_weight)
    incoming = swap(outgoing, 1)
    kept = call(
        down_kernel, jax.ShapeDtypeStruct((everyone, half), bfloat16), [SMEM, VMEM, VMEM], vmem=16,
        flops=2 * everyone * half * units,
    )(expert_info, act, down_weight)
    summed = (kept.astype(float32) + incoming.astype(float32)).reshape(far, near * tokens, half)
    back = summed[0]
    for k in range(1, far):
        back = back + swap(summed[k].astype(bfloat16), 0, k * near).astype(float32)
    back = back.reshape(near, tokens, half)
    result = back[0] + hiddens[0]
    for e in range(near):
        for k in range(outer):
            if k or e:
                result = result + swap(back[e].astype(bfloat16), k * cores, e).astype(float32)
    mine = result.astype(bfloat16)
    theirs = swap(mine, 1)
    output = jnp.where(
        core == 0, jnp.concatenate([mine, theirs], axis=1), jnp.concatenate([theirs, mine], axis=1)
    )
    return output.reshape(rows, steps, width)


def solution(mesh):
    return jax.shard_map(
        per_device,
        mesh=mesh,
        in_specs=(
            P("expert", None, None),
            P("expert", None, "pool", None),
            P("expert", None, None, None, None),
            P("pool", "expert", None, None, None, None),
            P("expert"),
            P(None, "expert"),
            P(None, "expert"),
            P("expert", None, None),
            P("expert", None, None),
            P("pool", None),
            P("expert", None, "pool"),
            P("expert", None, "pool"),
            P("expert", "pool", None),
        ),
        out_specs=P("expert", None, None),
        check_vma=False,
    )
```

time: 173 us -> 88.3 us (0.51)
  blocking collectives: 47 us -> 0 us
  waiting for transfers between devices: 73.9 us -> 35 us
  between operations: 13.7 us -> 0.23 us
  Pallas kernels: 0 us -> 11.6 us
  matrix products: 10.4 us -> 0 us
  starting transfers between devices: 9.81 us -> 19.7 us
  local copies, waits for them, and re-layouts: 15.2 us -> 19.9 us
    all_to_all x1 -> x0, blocking collectives: 41.5 us -> none  [per_device(): lax.all_to_all(outgoing_rows, 'expert', split_axis=0, concat_axis=0, tile...]
    ppermute x0 -> x22, waiting for transfers between devices: none -> 35 us  [swap(): return lax.ppermute(value, ('pool', 'expert'), pairs)]
    psum x1 -> x0, waiting for transfers between devices: 32.7 us -> none  [per_device(): lax.psum(projected.astype(jnp.bfloat16), 'pool').astype(jnp.float32)]
    reduce_scatter x1 -> x0, waiting for transfers between devices: 26.5 us -> none  [per_device(): lax.psum_scatter(partial_value.astype(jnp.float32).astype(jnp.bfloat16),...]
    ppermute x0 -> x22, starting transfers between devices: none -> 19.7 us  [swap(): return lax.ppermute(value, ('pool', 'expert'), pairs)]
    unnamed x26, local copies, waits for them, and re-layouts: 3.37 us -> 18.4 us
    all_to_all x2 -> x0, waiting for transfers between devices: 14.7 us -> none  [the longest x1 11.4 us: per_device(): lax.all_to_all(shares.astype(jnp.bfloat16), 'expert', split_axis=0, conca...]
    pallas_call x0 -> x5, Pallas kernels: none -> 11.6 us  [the longest x1 5.31 us: per_device(): pl.pallas_call(functools.partial(cache_kernel, heads, kv_heads, scale), o...]
  transfers between devices with their start and end apart: 4 -> 22, of which waited for: 4 -> 16; matrix products, arithmetic and copies ran while one was open for 3% -> 2% of each run, Pallas kernels for 0% -> 8%
where the time goes in v1:
time: 88.3 us; the launch traced here: 87.8 us
  waiting for transfers between devices  35 us (40%)
  local copies, waits for them, and re-layouts  19.9 us (23%)
  starting transfers between devices  19.7 us (22%)
  Pallas kernels  11.6 us (13%)
  other arithmetic  1.43 us (2%)
    ppermute x22, waiting for transfers between devices, swap(): return lax.ppermute(value, ('pool', 'expert'), pairs)  35 us
    ppermute x22, starting transfers between devices, swap(): return lax.ppermute(value, ('pool', 'expert'), pairs)  19.7 us
    unnamed x26, local copies, waits for them, and re-layouts  18.4 us
    pallas_call x1, Pallas kernels, per_device(): pl.pallas_call(functools.partial(cache_kernel, heads, kv_heads, scale), o...  5.31 us
    pallas_call x1, Pallas kernels, per_device(): call(functools.partial(page_kernel, heads, steps, page_size, scale, pool_...  2.44 us
    pallas_call x1, Pallas kernels, per_device(): call(functools.partial(expert_kernel, far), (jax.ShapeDtypeStruct((everyo...  2.25 us
  transfers between devices with their start and end apart: 22, of which 16 were waited for; matrix products, arithmetic and copies ran while one was open for 2% of the time, Pallas kernels for 8%

profile of v1, /device:TPU:0, one launch (start us, length us, event | category | flops | bytes accessed | tf_op | source)
XLA Modules:
  0.0 87.8 jit_solution(1046635297494511212)
XLA Ops:
  0.0 1.2 %constant_dynamic-slice_fusion = (bf16[4,1,64,1,2,128]{5,4,3,2,1,0:T(2,128)(2,1)S(1)}, bf16[4,1,64,1,2,128]{5,4,3,2,1,0:T(2,128)(2,1)S(1)}) fusion(bf16[4,1,64,2,2,128]{5,4,3,2,1,0:T(2,128)(2,1)} %param.16, s32[]{:T(128)S(6)} %select_n.72, s32[]{:T(128)S(6)} %select_n.70), kind=kLoop, calls=%fused_computation.20 | loop fusion | bytes 524296 | tf_op jit(solution)/shard_map/jit(dynamic_index_in_dim)/dynamic_slice | solution.py:190
  1.2 3.1 %collective-permute-start = (bf16[512,128]{1,0:T(8,128)(2,1)S(1)}, bf16[512,128]{1,0:T(8,128)(2,1)S(1)}, u32[]{:S(2)}, u32[]{:S(2)}) collective-permute-start(bf16[512,128]{1,0:T(8,128)(2,1)S(1)} %bitcast.25), channel_id=1, source_target_pairs={{0,16},{1,17},{2,18},{3,19},{4,20},{5,21},{6,22},{7,23},{8,24},{9,... | collective-permute-start | bytes 393224 | tf_op jit(solution)/shard_map/ppermute | solution.py:176
  4.3 0.0 collective-permute-start.1
  4.3 0.7 copy.16.page_row_ref
  5.0 0.7 copy.17.page_len_ref
  5.8 0.1 stack.32.info_ref
  5.8 1.9 %collective-permute-done.rest_1_ = bf16[512,128]{1,0:T(8,128)(2,1)S(1)} collective-permute-done((bf16[512,128]{1,0:T(8,128)(2,1)S(1)}, bf16[512,128]{1,0:T(8,128)(2,1)S(1)}, u32[]{:S(2)}, u32[]{:S(2)}) %collective-permute-start) | collective-permute-done | bytes 131104 | tf_op jit(solution)/shard_map/ppermute | solution.py:176
  7.8 0.0 collective-permute-start.2
  7.8 2.2 %copy-done.3 = bf16[8,512,2,2,128]{4,3,2,1,0:T(2,128)(2,1)S(1)} copy-done((bf16[8,512,2,2,128]{4,3,2,1,0:T(2,128)(2,1)S(1)}, bf16[8,512,2,2,128]{4,3,2,1,0:T(2,128)(2,1)}, u32[]{:S(2)}) %copy-start.3) | copy-done | bytes 4194328
  10.0 0.8 copy-done.6
  10.7 0.7 copy-done.8
  11.4 5.3 %shard_map.127 = (f32[8,16,128]{2,1,0:T(8,128)S(1)}, f32[8,16,128]{2,1,0:T(8,128)S(1)}, f32[8,16,128]{2,1,0:T(8,128)S(1)}) custom-call(s32[1]{0:T(128)} %bitcast.7.head_ref, s32[8]{0:T(128)S(1)} %copy-done.8, bf16[8,16,128]{2,1,0:T(8,128)(2,1)S(1)} %bitcast.20, bf16[8,2048,128]{2,1,0:T(8,128)(2,1)S(1)} %bitcast.17), custom_call_target="tpu_custom_call" | custom-call | flops 134217728 | bytes 4194304 | tf_op jit(solution)/shard_map/pallas_call | solution.py:210
  16.7 0.1 select_reduce_fusion
  16.8 0.0 collective-permute-done.1.rest_2_
  16.8 0.0 collective-permute-done.2.rest_3_
  16.9 0.0 copy-start
  16.9 3.4 %copy-done = bf16[1024,4096]{1,0:T(8,128)(2,1)S(1)} copy-done((bf16[1024,4096]{1,0:T(8,128)(2,1)S(1)}, bf16[1024,4096]{1,0:T(8,128)(2,1)}, u32[]{:S(2)}) %copy-start) | copy-done | bytes 8388632
  20.2 2.4 %shard_map.128 = (bf16[16,1024]{1,0:T(8,128)(2,1)S(1)}, bf16[16,2048]{1,0:T(8,128)(2,1)S(1)}) custom-call(s32[5]{0:T(128)S(1)} %stack.32.info_ref, s32[16,1]{1,0:T(8,128)S(1)} %copy.16.page_row_ref, s32[16,1]{1,0:T(8,128)S(1)} %copy.17.page_len_ref, bf16[128,128]{1,0:T(8,128)(2,1)S(1)} %bitcast.21, f32[128,128]{1,0:T(8,128)S(1)} %bitcast.22, ...), custom_call_target="tpu_custom_call" | custom-call | flops 67108864 | tf_op jit(solution)/shard_map/pallas_call | solution.py:224
  22.7 0.5 collective-permute-start.3
  23.2 0.1 reshape.68
  23.3 0.0 copy-start.1
  23.3 3.4 %copy-done.1 = bf16[1024,4096]{1,0:T(8,128)(2,1)S(1)} copy-done((bf16[1024,4096]{1,0:T(8,128)(2,1)S(1)}, bf16[1024,4096]{1,0:T(8,128)(2,1)}, u32[]{:S(2)}) %copy-start.1) | copy-done | bytes 8388632
  26.7 0.6 shard_map.129
  27.4 2.7 %collective-permute-start.6 = (bf16[16,2176]{1,0:T(8,128)(2,1)S(1)}, bf16[16,2176]{1,0:T(8,128)(2,1)S(1)}, u32[]{:S(2)}, u32[]{:S(2)}) collective-permute-start(bf16[16,2176]{1,0:T(8,128)(2,1)S(1)} %pad_maximum_fusion), channel_id=1, source_target_pairs={{0,17},{1,16},{2,19},{3,18},{4,21},{5,20},{6,23},{7,22},{8,25},{9,... | collective-permute-start | bytes 208904 | tf_op jit(solution)/shard_map/ppermute | solution.py:176
  30.1 0.5 collective-permute-start.5
  30.7 0.3 collective-permute-start.4
  30.9 2.0 %collective-permute-done.6 = bf16[16,2176]{1,0:T(8,128)(2,1)S(1)} collective-permute-done((bf16[16,2176]{1,0:T(8,128)(2,1)S(1)}, bf16[16,2176]{1,0:T(8,128)(2,1)S(1)}, u32[]{:S(2)}, u32[]{:S(2)}) %collective-permute-start.6) | collective-permute-done | bytes 69664 | tf_op jit(solution)/shard_map/ppermute | solution.py:176
  32.9 1.5 %collective-permute-done.5 = bf16[16,2176]{1,0:T(8,128)(2,1)S(1)} collective-permute-done((bf16[16,2176]{1,0:T(8,128)(2,1)S(1)}, bf16[16,2176]{1,0:T(8,128)(2,1)S(1)}, u32[]{:S(2)}, u32[]{:S(2)}) %collective-permute-start.5) | collective-permute-done | bytes 69664 | tf_op jit(solution)/shard_map/ppermute | solution.py:176
  34.5 0.5 collective-permute-done.4
  35.0 3.7 %collective-permute-start.9 = (bf16[32,2176]{1,0:T(8,128)(2,1)S(1)}, bf16[32,2176]{1,0:T(8,128)(2,1)S(1)}, u32[]{:S(2)}, u32[]{:S(2)}) collective-permute-start(bf16[32,2176]{1,0:T(8,128)(2,1)S(1)} %maximum_maximum_fusion.rest_0_), channel_id=1, source_target_pairs={{0,6},{1,7},{2,4},{3,5},{4,2},{5,3},{6,0},{7,1},{8,14},{9,15},{10,... | collective-permute-start | bytes 417800 | tf_op jit(solution)/shard_map/ppermute | solution.py:176
  38.7 0.8 collective-permute-start.7
  39.5 4.0 %collective-permute-done.9.rest_3_ = bf16[32,2176]{1,0:T(8,128)(2,1)S(1)} collective-permute-done((bf16[32,2176]{1,0:T(8,128)(2,1)S(1)}, bf16[32,2176]{1,0:T(8,128)(2,1)S(1)}, u32[]{:S(2)}, u32[]{:S(2)}) %collective-permute-start.9) | collective-permute-done | bytes 139296 | tf_op jit(solution)/shard_map/ppermute | solution.py:176
  43.4 6.1 %collective-permute-done.8.rest_2_ = bf16[32,2176]{1,0:T(8,128)(2,1)S(1)} collective-permute-done((bf16[32,2176]{1,0:T(8,128)(2,1)S(1)}, bf16[32,2176]{1,0:T(8,128)(2,1)S(1)}, u32[]{:S(2)}, u32[]{:S(2)}) %collective-permute-start.8) | collective-permute-done | bytes 139296 | tf_op jit(solution)/shard_map/ppermute | solution.py:176
  49.6 0.5 collective-permute-start.11
  50.1 0.1 pad_add_fusion.info_ref
  50.2 0.8 collective-permute-done.12.rest_6_
  50.9 0.2 collective-permute-done.11.rest_5_
  51.1 2.2 %copy-done.2 = bf16[2,256,4096]{2,1,0:T(8,128)(2,1)S(1)} copy-done((bf16[2,256,4096]{2,1,0:T(8,128)(2,1)S(1)}, bf16[2,256,4096]{2,1,0:T(8,128)(2,1)}, u32[]{:S(2)}) %copy-start.2) | copy-done | bytes 4194328
  53.3 2.2 %copy-done.4 = bf16[2,4096,256]{2,1,0:T(8,128)(2,1)S(1)} copy-done((bf16[2,4096,256]{2,1,0:T(8,128)(2,1)S(1)}, bf16[2,4096,256]{2,1,0:T(8,128)(2,1)}, u32[]{:S(2)}) %copy-start.4) | copy-done | bytes 4194328
  55.5 2.2 %copy-done.5 = bf16[2,4096,256]{2,1,0:T(8,128)(2,1)S(1)} copy-done((bf16[2,4096,256]{2,1,0:T(8,128)(2,1)S(1)}, bf16[2,4096,256]{2,1,0:T(8,128)(2,1)}, u32[]{:S(2)}) %copy-start.5) | copy-done | bytes 4194328
  57.7 2.3 %shard_map.130 = (bf16[128,512]{1,0:T(8,128)(2,1)S(1)}, bf16[128,2048]{1,0:T(8,128)(2,1)S(1)}) custom-call(s32[3]{0:T(128)S(1)} %pad_add_fusion.info_ref, bf16[32,2176]{1,0:T(8,128)(2,1)S(1)} %maximum_maximum_fusion.rest_0_, bf16[32,2176]{1,0:T(8,128)(2,1)S(1)} %collective-permute-done.7.rest_1_, bf16[32,2176]{1,0:T(8,128)(2,1)S(1)} %collective-permute-done.8.rest_2_, ...), custom_call_target="tpu_custom_call" | custom-call | flops 1073741824 | tf_op jit(solution)/shard_map/pallas_call | solution.py:273
  59.9 0.4 collective-permute-start.14
  60.3 1.0 %shard_map.131 = bf16[128,2048]{1,0:T(8,128)(2,1)S(1)} custom-call(s32[3]{0:T(128)S(1)} %pad_add_fusion.info_ref, bf16[128,512]{1,0:T(8,128)(2,1)S(1)} %get-tuple-element.17.act_ref, bf16[2,256,4096]{2,1,0:T(8,128)(2,1)S(1)} %copy-done.2), custom_call_target="tpu_custom_call" | custom-call | flops 268435456 | tf_op jit(solution)/shard_map/pallas_call | solution.py:284
  61.3 0.6 collective-permute-done.14
  61.9 0.2 fusion.5
  62.1 0.1 collective-permute-start.15
  62.2 2.5 %collective-permute-start.17 = (bf16[32,2048]{1,0:T(8,128)(2,1)S(1)}, bf16[32,2048]{1,0:T(8,128)(2,1)S(1)}, u32[]{:S(2)}, u32[]{:S(2)}) collective-permute-start(bf16[32,2048]{1,0:T(8,128)(2,1)S(1)} %get-tuple-element.22), channel_id=1, source_target_pairs={{0,6},{1,7},{2,4},{3,5},{4,2},{5,3},{6,0},{7,1},{8,14},{9,15},{10,... | collective-permute-start | bytes 393224 | tf_op jit(solution)/shard_map/ppermute | solution.py:176
  64.7 0.9 %collective-permute-start.16 = (bf16[32,2048]{1,0:T(8,128)(2,1)S(1)}, bf16[32,2048]{1,0:T(8,128)(2,1)S(1)}, u32[]{:S(2)}, u32[]{:S(2)}) collective-permute-start(bf16[32,2048]{1,0:T(8,128)(2,1)S(1)} %get-tuple-element.23), channel_id=1, source_target_pairs={{0,4},{1,5},{2,6},{3,7},{4,0},{5,1},{6,2},{7,3},{8,12},{9,13},{10,... | collective-permute-start | bytes 393224 | tf_op jit(solution)/shard_map/ppermute | solution.py:176
  65.7 2.2 %collective-permute-done.15 = bf16[32,2048]{1,0:T(8,128)(2,1)S(1)} collective-permute-done((bf16[32,2048]{1,0:T(8,128)(2,1)S(1)}, bf16[32,2048]{1,0:T(8,128)(2,1)S(1)}, u32[]{:S(2)}, u32[]{:S(2)}) %collective-permute-start.15) | collective-permute-done | bytes 131104 | tf_op jit(solution)/shard_map/ppermute | solution.py:176
  67.9 4.0 %collective-permute-done.17 = bf16[32,2048]{1,0:T(8,128)(2,1)S(1)} collective-permute-done((bf16[32,2048]{1,0:T(8,128)(2,1)S(1)}, bf16[32,2048]{1,0:T(8,128)(2,1)S(1)}, u32[]{:S(2)}, u32[]{:S(2)}) %collective-permute-start.17) | collective-permute-done | bytes 131104 | tf_op jit(solution)/shard_map/ppermute | solution.py:176
  71.9 5.6 %collective-permute-done.16 = bf16[32,2048]{1,0:T(8,128)(2,1)S(1)} collective-permute-done((bf16[32,2048]{1,0:T(8,128)(2,1)S(1)}, bf16[32,2048]{1,0:T(8,128)(2,1)S(1)}, u32[]{:S(2)}, u32[]{:S(2)}) %collective-permute-start.16) | collective-permute-done | bytes 131104 | tf_op jit(solution)/shard_map/ppermute | solution.py:176
  77.5 0.1 fusion.1
  77.6 1.4 %collective-permute-start.18 = (bf16[16,2048]{1,0:T(8,128)(2,1)S(1)}, bf16[16,2048]{1,0:T(8,128)(2,1)S(1)}, u32[]{:S(2)}, u32[]{:S(2)}) collective-permute-start(bf16[16,2048]{1,0:T(8,128)(2,1)S(1)} %get-tuple-element.24), channel_id=1, source_target_pairs={{0,16},{1,17},{2,18},{3,19},{4,20},{5,21},{6,22},{7,23},{8,24},{9,... | collective-permute-start | bytes 196616 | tf_op jit(solution)/shard_map/ppermute | solution.py:176
  79.0 1.4 %collective-permute-start.19 = (bf16[16,2048]{1,0:T(8,128)(2,1)S(1)}, bf16[16,2048]{1,0:T(8,128)(2,1)S(1)}, u32[]{:S(2)}, u32[]{:S(2)}) collective-permute-start(bf16[16,2048]{1,0:T(8,128)(2,1)S(1)} %get-tuple-element.25), channel_id=1, source_target_pairs={{0,1},{1,0},{2,3},{3,2},{4,5},{5,4},{6,7},{7,6},{8,9},{9,8},{10,11... | collective-permute-start | bytes 196616 | tf_op jit(solution)/shard_map/ppermute | solution.py:176
  80.3 0.8 collective-permute-start.20
  81.1 0.8 collective-permute-done.18
  81.9 1.6 %collective-permute-done.19 = bf16[16,2048]{1,0:T(8,128)(2,1)S(1)} collective-permute-done((bf16[16,2048]{1,0:T(8,128)(2,1)S(1)}, bf16[16,2048]{1,0:T(8,128)(2,1)S(1)}, u32[]{:S(2)}, u32[]{:S(2)}) %collective-permute-start.19) | collective-permute-done | bytes 65568 | tf_op jit(solution)/shard_map/ppermute | solution.py:176
  83.5 2.0 %collective-permute-done.20 = bf16[16,2048]{1,0:T(8,128)(2,1)S(1)} collective-permute-done((bf16[16,2048]{1,0:T(8,128)(2,1)S(1)}, bf16[16,2048]{1,0:T(8,128)(2,1)S(1)}, u32[]{:S(2)}, u32[]{:S(2)}) %collective-permute-start.20) | collective-permute-done | bytes 65568 | tf_op jit(solution)/shard_map/ppermute | solution.py:176
  85.5 0.1 add_convert_fusion
  85.6 0.1 collective-permute-start.21
  85.7 0.1 concatenate.29
  85.7 1.2 %collective-permute-done.21 = bf16[16,2048]{1,0:T(8,128)(2,1)S(1)} collective-permute-done((bf16[16,2048]{1,0:T(8,128)(2,1)S(1)}, bf16[16,2048]{1,0:T(8,128)(2,1)S(1)}, u32[]{:S(2)}, u32[]{:S(2)}) %collective-permute-start.21) | collective-permute-done | bytes 65568 | tf_op jit(solution)/shard_map/ppermute | solution.py:176
  86.9 0.1 concatenate.30
  86.9 0.9 broadcast_select_fusion
  (33 shorter events, 0.2 us)
Async XLA Ops:
  0.0 16.9 %copy-start.7 = (bf16[8,2,8,128]{3,2,1,0:T(8,128)(2,1)S(1)}, bf16[8,2,8,128]{3,2,1,0:T(8,128)(2,1)}, u32[]{:S(2)}) copy-start(bf16[8,2,8,128]{3,2,1,0:T(8,128)(2,1)} %param.14) | copy-start | bytes 98308
  0.0 16.7 %copy-start.10 = (f32[8,2,8]{2,1,0:T(2,128)S(1)}, f32[8,2,8]{2,1,0:T(2,128)}, u32[]{:S(2)}) copy-start(f32[8,2,8]{2,1,0:T(2,128)} %param.21) | copy-start | bytes 1540
  0.0 16.7 %copy-start.11 = (s32[8,2,8]{2,1,0:T(2,128)S(1)}, s32[8,2,8]{2,1,0:T(2,128)}, u32[]{:S(2)}) copy-start(s32[8,2,8]{2,1,0:T(2,128)} %param.20) | copy-start | bytes 1540
  1.2 6.6 %collective-permute-start = (bf16[512,128]{1,0:T(8,128)(2,1)S(1)}, bf16[512,128]{1,0:T(8,128)(2,1)S(1)}, u32[]{:S(2)}, u32[]{:S(2)}) collective-permute-start(bf16[512,128]{1,0:T(8,128)(2,1)S(1)} %bitcast.25), channel_id=1, source_target_pairs={{0,16},{1,17},{2,18},{3,19},{4,20},{5,21},{6,22},{7,23},{8,24},{9,... | collective-permute-start | bytes 393224 | tf_op jit(solution)/shard_map/ppermute | solution.py:176
  4.3 12.6 %collective-permute-start.1 = (bf16[512,128]{1,0:T(8,128)(2,1)S(1)}, bf16[512,128]{1,0:T(8,128)(2,1)S(1)}, u32[]{:S(2)}, u32[]{:S(2)}) collective-permute-start(bf16[512,128]{1,0:T(8,128)(2,1)S(1)} %bitcast.18), channel_id=1, source_target_pairs={{0,8},{1,9},{2,10},{3,11},{4,12},{5,13},{6,14},{7,15},{8,0},{9,1},... | collective-permute-start | bytes 393224 | tf_op jit(solution)/shard_map/ppermute | solution.py:176
  7.8 9.1 %collective-permute-start.2 = (bf16[512,128]{1,0:T(8,128)(2,1)S(1)}, bf16[512,128]{1,0:T(8,128)(2,1)S(1)}, u32[]{:S(2)}, u32[]{:S(2)}) collective-permute-start(bf16[512,128]{1,0:T(8,128)(2,1)S(1)} %collective-permute-done.rest_1_), channel_id=1, source_target_pairs={{0,8},{1,9},{2,10},{3,11},{4,12},{5,13},{6,14},{7,15},{8,0},{9,1},... | collective-permute-start | bytes 393224 | tf_op jit(solution)/shard_map/ppermute | solution.py:176
  7.8 2.2 %copy-start.3 = (bf16[8,512,2,2,128]{4,3,2,1,0:T(2,128)(2,1)S(1)}, bf16[8,512,2,2,128]{4,3,2,1,0:T(2,128)(2,1)}, u32[]{:S(2)}) copy-start(bf16[8,512,2,2,128]{4,3,2,1,0:T(2,128)(2,1)} %param.15) | copy-start | bytes 12582916
  10.0 0.8 copy-start.6
  10.7 0.7 copy-start.8
  16.9 3.4 %copy-start = (bf16[1024,4096]{1,0:T(8,128)(2,1)S(1)}, bf16[1024,4096]{1,0:T(8,128)(2,1)}, u32[]{:S(2)}) copy-start(bf16[1024,4096]{1,0:T(8,128)(2,1)} %weight_ref.1) | copy-start | bytes 25165828
  20.2 3.0 %copy-start.9 = (bf16[8,2,4096]{2,1,0:T(2,128)(2,1)S(1)}, bf16[8,2,4096]{2,1,0:T(2,128)(2,1)}, u32[]{:S(2)}) copy-start(bf16[8,2,4096]{2,1,0:T(2,128)(2,1)} %param.13) | copy-start | bytes 393220
  22.7 4.6 %collective-permute-start.3 = (bf16[16,2048]{1,0:T(8,128)(2,1)S(1)}, bf16[16,2048]{1,0:T(8,128)(2,1)S(1)}, u32[]{:S(2)}, u32[]{:S(2)}) collective-permute-start(bf16[16,2048]{1,0:T(8,128)(2,1)S(1)} %get-tuple-element.16), channel_id=1, source_target_pairs={{0,8},{1,9},{2,10},{3,11},{4,12},{5,13},{6,14},{7,15},{8,0},{9,1},... | collective-permute-start | bytes 196616 | tf_op jit(solution)/shard_map/ppermute | solution.py:176
  23.3 3.4 %copy-start.1 = (bf16[1024,4096]{1,0:T(8,128)(2,1)S(1)}, bf16[1024,4096]{1,0:T(8,128)(2,1)}, u32[]{:S(2)}) copy-start(bf16[1024,4096]{1,0:T(8,128)(2,1)} %weight_ref.1) | copy-start | bytes 25165828
  27.4 5.5 %collective-permute-start.6 = (bf16[16,2176]{1,0:T(8,128)(2,1)S(1)}, bf16[16,2176]{1,0:T(8,128)(2,1)S(1)}, u32[]{:S(2)}, u32[]{:S(2)}) collective-permute-start(bf16[16,2176]{1,0:T(8,128)(2,1)S(1)} %pad_maximum_fusion), channel_id=1, source_target_pairs={{0,17},{1,16},{2,19},{3,18},{4,21},{5,20},{6,23},{7,22},{8,25},{9,... | collective-permute-start | bytes 208904 | tf_op jit(solution)/shard_map/ppermute | solution.py:176
  30.1 4.3 %collective-permute-start.5 = (bf16[16,2176]{1,0:T(8,128)(2,1)S(1)}, bf16[16,2176]{1,0:T(8,128)(2,1)S(1)}, u32[]{:S(2)}, u32[]{:S(2)}) collective-permute-start(bf16[16,2176]{1,0:T(8,128)(2,1)S(1)} %pad_maximum_fusion), channel_id=1, source_target_pairs={{0,1},{1,0},{2,3},{3,2},{4,5},{5,4},{6,7},{7,6},{8,9},{9,8},{10,11... | collective-permute-start | bytes 208904 | tf_op jit(solution)/shard_map/ppermute | solution.py:176
  30.7 4.3 %collective-permute-start.4 = (bf16[16,2176]{1,0:T(8,128)(2,1)S(1)}, bf16[16,2176]{1,0:T(8,128)(2,1)S(1)}, u32[]{:S(2)}, u32[]{:S(2)}) collective-permute-start(bf16[16,2176]{1,0:T(8,128)(2,1)S(1)} %pad_maximum_fusion), channel_id=1, source_target_pairs={{0,16},{1,17},{2,18},{3,19},{4,20},{5,21},{6,22},{7,23},{8,24},{9,... | collective-permute-start | bytes 208904 | tf_op jit(solution)/shard_map/ppermute | solution.py:176
  35.0 8.4 %collective-permute-start.9 = (bf16[32,2176]{1,0:T(8,128)(2,1)S(1)}, bf16[32,2176]{1,0:T(8,128)(2,1)S(1)}, u32[]{:S(2)}, u32[]{:S(2)}) collective-permute-start(bf16[32,2176]{1,0:T(8,128)(2,1)S(1)} %maximum_maximum_fusion.rest_0_), channel_id=1, source_target_pairs={{0,6},{1,7},{2,4},{3,5},{4,2},{5,3},{6,0},{7,1},{8,14},{9,15},{10,... | collective-permute-start | bytes 417800 | tf_op jit(solution)/shard_map/ppermute | solution.py:176
  38.7 10.9 %collective-permute-start.8 = (bf16[32,2176]{1,0:T(8,128)(2,1)S(1)}, bf16[32,2176]{1,0:T(8,128)(2,1)S(1)}, u32[]{:S(2)}, u32[]{:S(2)}) collective-permute-start(bf16[32,2176]{1,0:T(8,128)(2,1)S(1)} %maximum_maximum_fusion.rest_0_), channel_id=1, source_target_pairs={{0,4},{1,5},{2,6},{3,7},{4,0},{5,1},{6,2},{7,3},{8,12},{9,13},{10,... | collective-permute-start | bytes 417800 | tf_op jit(solution)/shard_map/ppermute | solution.py:176
  38.7 10.9 %collective-permute-start.7 = (bf16[32,2176]{1,0:T(8,128)(2,1)S(1)}, bf16[32,2176]{1,0:T(8,128)(2,1)S(1)}, u32[]{:S(2)}, u32[]{:S(2)}) collective-permute-start(bf16[32,2176]{1,0:T(8,128)(2,1)S(1)} %maximum_maximum_fusion.rest_0_), channel_id=1, source_target_pairs={{0,2},{1,3},{2,0},{3,1},{4,6},{5,7},{6,4},{7,5},{8,10},{9,11},{10,... | collective-permute-start | bytes 417800 | tf_op jit(solution)/shard_map/ppermute | solution.py:176
  39.5 10.7 %collective-permute-start.10 = (bf16[32,2176]{1,0:T(8,128)(2,1)S(1)}, bf16[32,2176]{1,0:T(8,128)(2,1)S(1)}, u32[]{:S(2)}, u32[]{:S(2)}) collective-permute-start(bf16[32,2176]{1,0:T(8,128)(2,1)S(1)} %maximum_maximum_fusion.rest_0_), channel_id=1, source_target_pairs={{0,8},{1,9},{2,10},{3,11},{4,12},{5,13},{6,14},{7,15},{8,0},{9,1},... | collective-permute-start | bytes 417800 | tf_op jit(solution)/shard_map/ppermute | solution.py:176
  43.4 6.7 %collective-permute-start.13 = (bf16[32,2176]{1,0:T(8,128)(2,1)S(1)}, bf16[32,2176]{1,0:T(8,128)(2,1)S(1)}, u32[]{:S(2)}, u32[]{:S(2)}) collective-permute-start(bf16[32,2176]{1,0:T(8,128)(2,1)S(1)} %collective-permute-done.9.rest_3_), channel_id=1, source_target_pairs={{0,8},{1,9},{2,10},{3,11},{4,12},{5,13},{6,14},{7,15},{8,0},{9,1},... | collective-permute-start | bytes 417800 | tf_op jit(solution)/shard_map/ppermute | solution.py:176
  49.6 1.4 %collective-permute-start.12 = (bf16[32,2176]{1,0:T(8,128)(2,1)S(1)}, bf16[32,2176]{1,0:T(8,128)(2,1)S(1)}, u32[]{:S(2)}, u32[]{:S(2)}) collective-permute-start(bf16[32,2176]{1,0:T(8,128)(2,1)S(1)} %collective-permute-done.8.rest_2_), channel_id=1, source_target_pairs={{0,8},{1,9},{2,10},{3,11},{4,12},{5,13},{6,14},{7,15},{8,0},{9,1},... | collective-permute-start | bytes 417800 | tf_op jit(solution)/shard_map/ppermute | solution.py:176
  49.6 1.6 %collective-permute-start.11 = (bf16[32,2176]{1,0:T(8,128)(2,1)S(1)}, bf16[32,2176]{1,0:T(8,128)(2,1)S(1)}, u32[]{:S(2)}, u32[]{:S(2)}) collective-permute-start(bf16[32,2176]{1,0:T(8,128)(2,1)S(1)} %collective-permute-done.7.rest_1_), channel_id=1, source_target_pairs={{0,8},{1,9},{2,10},{3,11},{4,12},{5,13},{6,14},{7,15},{8,0},{9,1},... | collective-permute-start | bytes 417800 | tf_op jit(solution)/shard_map/ppermute | solution.py:176
  51.1 2.2 %copy-start.2 = (bf16[2,256,4096]{2,1,0:T(8,128)(2,1)S(1)}, bf16[2,256,4096]{2,1,0:T(8,128)(2,1)}, u32[]{:S(2)}) copy-start(bf16[2,256,4096]{2,1,0:T(8,128)(2,1)} %down_ref.1) | copy-start | bytes 12582916
  53.3 2.2 %copy-start.4 = (bf16[2,4096,256]{2,1,0:T(8,128)(2,1)S(1)}, bf16[2,4096,256]{2,1,0:T(8,128)(2,1)}, u32[]{:S(2)}) copy-start(bf16[2,4096,256]{2,1,0:T(8,128)(2,1)} %rest_8_.1) | copy-start | bytes 12582916
  55.5 2.2 %copy-start.5 = (bf16[2,4096,256]{2,1,0:T(8,128)(2,1)S(1)}, bf16[2,4096,256]{2,1,0:T(8,128)(2,1)}, u32[]{:S(2)}) copy-start(bf16[2,4096,256]{2,1,0:T(8,128)(2,1)} %rest_9_.1) | copy-start | bytes 12582916
  59.9 2.0 %collective-permute-start.14 = (bf16[128,2048]{1,0:T(8,128)(2,1)S(1)}, bf16[128,2048]{1,0:T(8,128)(2,1)S(1)}, u32[]{:S(2)}, u32[]{:S(2)}) collective-permute-start(bf16[128,2048]{1,0:T(8,128)(2,1)S(1)} %get-tuple-element.18), channel_id=1, source_target_pairs={{0,8},{1,9},{2,10},{3,11},{4,12},{5,13},{6,14},{7,15},{8,0},{9,1},... | collective-permute-start | bytes 1572872 | tf_op jit(solution)/shard_map/ppermute | solution.py:176
  62.1 5.8 %collective-permute-start.15 = (bf16[32,2048]{1,0:T(8,128)(2,1)S(1)}, bf16[32,2048]{1,0:T(8,128)(2,1)S(1)}, u32[]{:S(2)}, u32[]{:S(2)}) collective-permute-start(bf16[32,2048]{1,0:T(8,128)(2,1)S(1)} %get-tuple-element.21), channel_id=1, source_target_pairs={{0,2},{1,3},{2,0},{3,1},{4,6},{5,7},{6,4},{7,5},{8,10},{9,11},{10,... | collective-permute-start | bytes 393224 | tf_op jit(solution)/shard_map/ppermute | solution.py:176
  62.2 9.7 %collective-permute-start.17 = (bf16[32,2048]{1,0:T(8,128)(2,1)S(1)}, bf16[32,2048]{1,0:T(8,128)(2,1)S(1)}, u32[]{:S(2)}, u32[]{:S(2)}) collective-permute-start(bf16[32,2048]{1,0:T(8,128)(2,1)S(1)} %get-tuple-element.22), channel_id=1, source_target_pairs={{0,6},{1,7},{2,4},{3,5},{4,2},{5,3},{6,0},{7,1},{8,14},{9,15},{10,... | collective-permute-start | bytes 393224 | tf_op jit(solution)/shard_map/ppermute | solution.py:176
  64.7 12.8 %collective-permute-start.16 = (bf16[32,2048]{1,0:T(8,128)(2,1)S(1)}, bf16[32,2048]{1,0:T(8,128)(2,1)S(1)}, u32[]{:S(2)}, u32[]{:S(2)}) collective-permute-start(bf16[32,2048]{1,0:T(8,128)(2,1)S(1)} %get-tuple-element.23), channel_id=1, source_target_pairs={{0,4},{1,5},{2,6},{3,7},{4,0},{5,1},{6,2},{7,3},{8,12},{9,13},{10,... | collective-permute-start | bytes 393224 | tf_op jit(solution)/shard_map/ppermute | solution.py:176
  77.6 4.3 %collective-permute-start.18 = (bf16[16,2048]{1,0:T(8,128)(2,1)S(1)}, bf16[16,2048]{1,0:T(8,128)(2,1)S(1)}, u32[]{:S(2)}, u32[]{:S(2)}) collective-permute-start(bf16[16,2048]{1,0:T(8,128)(2,1)S(1)} %get-tuple-element.24), channel_id=1, source_target_pairs={{0,16},{1,17},{2,18},{3,19},{4,20},{5,21},{6,22},{7,23},{8,24},{9,... | collective-permute-start | bytes 196616 | tf_op jit(solution)/shard_map/ppermute | solution.py:176
  79.0 4.5 %collective-permute-start.19 = (bf16[16,2048]{1,0:T(8,128)(2,1)S(1)}, bf16[16,2048]{1,0:T(8,128)(2,1)S(1)}, u32[]{:S(2)}, u32[]{:S(2)}) collective-permute-start(bf16[16,2048]{1,0:T(8,128)(2,1)S(1)} %get-tuple-element.25), channel_id=1, source_target_pairs={{0,1},{1,0},{2,3},{3,2},{4,5},{5,4},{6,7},{7,6},{8,9},{9,8},{10,11... | collective-permute-start | bytes 196616 | tf_op jit(solution)/shard_map/ppermute | solution.py:176
  80.3 5.2 %collective-permute-start.20 = (bf16[16,2048]{1,0:T(8,128)(2,1)S(1)}, bf16[16,2048]{1,0:T(8,128)(2,1)S(1)}, u32[]{:S(2)}, u32[]{:S(2)}) collective-permute-start(bf16[16,2048]{1,0:T(8,128)(2,1)S(1)} %get-tuple-element.25), channel_id=1, source_target_pairs={{0,17},{1,16},{2,19},{3,18},{4,21},{5,20},{6,23},{7,22},{8,25},{9,... | collective-permute-start | bytes 196616 | tf_op jit(solution)/shard_map/ppermute | solution.py:176
  85.6 1.3 %collective-permute-start.21 = (bf16[16,2048]{1,0:T(8,128)(2,1)S(1)}, bf16[16,2048]{1,0:T(8,128)(2,1)S(1)}, u32[]{:S(2)}, u32[]{:S(2)}) collective-permute-start(bf16[16,2048]{1,0:T(8,128)(2,1)S(1)} %add_convert_fusion), channel_id=1, source_target_pairs={{0,8},{1,9},{2,10},{3,11},{4,12},{5,13},{6,14},{7,15},{8,0},{9,1},... | collective-permute-start | bytes 196616 | tf_op jit(solution)/shard_map/ppermute | solution.py:176

commit v2 on v1

v2 whole, which is shorter than its diff:
```python
import functools
import math

import jax
import jax.numpy as jnp
from jax import lax
from jax.experimental import pallas as pl
from jax.experimental.pallas import tpu as pltpu
from jax.sharding import PartitionSpec as P

MIB = 1 << 20
LANES = 128
very_low = -1e30
VMEM = pl.BlockSpec(memory_space=pltpu.VMEM)
SMEM = pl.BlockSpec(memory_space=pltpu.SMEM)
HBM = pl.BlockSpec(memory_space=pltpu.HBM)
ANY = pl.BlockSpec(memory_space=pl.ANY)
float32 = jnp.float32
bfloat16 = jnp.bfloat16


def far_off(array):
    return pltpu.with_memory_space_constraint(array, pltpu.HBM)


def dot_t(a, b):
    return lax.dot_general(a, b, (((1,), (1,)), ((), ())), preferred_element_type=float32)


def dot(a, b):
    return jnp.dot(a, b, preferred_element_type=float32)


def add_pages(scale, group, sets, first_pages, row_ref, len_ref, q_ref, acc_ref, top_ref, total_ref):
    parts = []
    for pages, first in zip(sets, first_pages):
        held, span = len_ref.shape[0] // first[1], None
        span = pages.shape[0] // held
        for i in range(held):
            page = first[0] * held + i
            rows = pl.ds(pl.multiple_of(row_ref[page] * group, group), group)
            kv = pages[i * span : (i + 1) * span, :]
            scores = dot_t(q_ref[rows, :], kv) * scale
            lane = lax.broadcasted_iota(jnp.int32, scores.shape, 1)
            seen = (lane // 2 < len_ref[page]) & (lane % 2 == 0)
            scores = jnp.where(seen, scores, very_low)
            top = jnp.max(scores, axis=1, keepdims=True)
            weights = jnp.where(seen, jnp.exp(scores - top), 0.0)
            total = jnp.sum(weights, axis=1, keepdims=True)
            acc = dot(pltpu.roll(weights, 1, 1).astype(bfloat16), kv)
            parts.append((rows, top, total, acc))
    before = top_ref[...]
    for rows, top, _, _ in parts:
        top_ref[rows, :] = jnp.maximum(top_ref[rows, :], top)
    shrink = jnp.exp(before - top_ref[...])
    acc_ref[...] = acc_ref[...] * shrink
    total_ref[...] = total_ref[...] * shrink
    for rows, top, total, acc in parts:
        factor = jnp.exp(top - top_ref[rows, :])
        acc_ref[rows, :] += acc * factor
        total_ref[rows, :] += total * factor


def cache_kernel(
    heads, kv_heads, pool_size, scale, info_ref, len_ref, row_ref, size_ref, q_hbm, own_ref, kv_hbm, weight_hbm, residual_hbm,
    acc_ref, top_ref, total_ref, send_ref, keep_ref, residual_ref, kv_ref, q_ref, kv_sem, weight_sem, q_sem,
):
    rows = kv_hbm.shape[0]
    q_copy = pltpu.make_async_copy(q_hbm, q_ref, q_sem.at[0])
    q_copy.start()
    copies = [pltpu.make_async_copy(kv_hbm.at[r], kv_ref.at[r], kv_sem.at[r]) for r in range(rows)]
    for copy in copies:
        copy.start()
    chunks = weight_sem.shape[1]
    deep = weight_hbm.shape[0] // chunks
    half = send_ref.shape[1]
    weights_in = []
    for side, target in enumerate((send_ref, keep_ref)):
        which = info_ref[0] if side else 1 - info_ref[0]
        columns = pl.ds(pl.multiple_of(which * half, half), half)
        for n in range(chunks):
            part = pl.ds(n * deep, deep)
            weights_in.append(
                pltpu.make_async_copy(weight_hbm.at[part, columns], target.at[part], weight_sem.at[side, n])
            )
    mine = pl.ds(pl.multiple_of(info_ref[0] * half, half), half)
    weights_in.append(pltpu.make_async_copy(residual_hbm.at[:, mine], residual_ref, q_sem.at[1]))
    for copy in weights_in:
        copy.start()
    q_copy.wait()
    group = q_ref.shape[0] // rows
    wide = 2 * kv_heads
    for r in range(rows):
        copies[r].wait()
        kv = kv_ref[r]
        here = slice(r * group, (r + 1) * group)
        scores = dot_t(q_ref[here, :], kv) * scale
        lane = lax.broadcasted_iota(jnp.int32, scores.shape, 1)
        token = lax.broadcasted_iota(jnp.int32, scores.shape, 0) // heads
        seen = (lane // wide <= len_ref[r] + token) & (lane % wide == 2 * info_ref[4])
        scores = jnp.where(seen, scores, very_low)
        top = jnp.max(scores, axis=1, keepdims=True)
        weights = jnp.where(seen, jnp.exp(scores - top), 0.0)
        total = jnp.sum(weights, axis=1, keepdims=True)
        acc_ref[here, :] = dot(pltpu.roll(weights, 1, 1).astype(bfloat16), kv)
        top_ref[here, :] = jnp.broadcast_to(top, (group, top_ref.shape[1]))
        total_ref[here, :] = jnp.broadcast_to(total, (group, total_ref.shape[1]))
    add_pages(
        scale, group, [own_ref], [(info_ref[5], pool_size)], row_ref, size_ref, q_ref, acc_ref, top_ref, total_ref
    )
    for copy in weights_in:
        copy.wait()


def page_kernel(
    heads, group, pool_size, scale, info_ref, row_ref, size_ref, q_ref, acc_in, top_in, total_in, *rest
):
    count = pool_size - 1
    pages = rest[:count]
    weight_ref, low_ref, send_ref, acc_ref, top_ref, total_ref = rest[count:]
    acc_ref[...] = acc_in[...]
    top_ref[...] = top_in[...]
    total_ref[...] = total_in[...]
    firsts = [(info_ref[6 + n], pool_size) for n in range(count)]
    add_pages(scale, group, pages, firsts, row_ref, size_ref, q_ref, acc_ref, top_ref, total_ref)
    acc_ref[...] = acc_ref[...] / total_ref[...]
    tokens = acc_ref.shape[0] // heads
    low = jnp.concatenate(
        [acc_ref[pl.ds(h, tokens, stride=heads), :].astype(bfloat16) for h in range(heads)], axis=1
    )
    low_ref[...] = low
    send_ref[...] = dot(low, weight_ref[...]).astype(bfloat16)


def load_kernel(count, *refs):
    sources, dests, sems = refs[1 : 1 + count], refs[1 + count : 1 + 2 * count], refs[-1]
    chunks = sems.shape[1]
    copies = []
    for n in range(count):
        for j in range(sources[n].shape[0]):
            size = sources[n].shape[1] // chunks
            for i in range(chunks):
                part = pl.ds(i * size, size)
                copies.append(
                    pltpu.make_async_copy(sources[n].at[j, part], dests[n].at[j, part], sems.at[n, i, j])
                )
    for copy in copies:
        copy.start()
    for copy in copies:
        copy.wait()


def project_kernel(info_ref, low_ref, weight_ref, residual_ref, keep_ref):
    first = info_ref[1].astype(float32)
    keep_ref[...] = dot(low_ref[...], weight_ref[...]) + residual_ref[...].astype(float32) * first


def expert_kernel(count, info_ref, *rest):
    own, other = rest[:count], rest[count : 2 * count]
    gate_ref, up_ref, down_ref, act_ref, send_ref = rest[2 * count :]
    half = send_ref.shape[1]
    own_all = jnp.concatenate([r[...] for r in own], axis=0)
    other_all = jnp.concatenate([r[:, :half] for r in other], axis=0)
    table = own_all[:, half:].astype(float32)
    own_all = own_all[:, :half]
    lane = lax.broadcasted_iota(jnp.int32, table.shape, 1)
    core = info_ref[0]
    first = pl.ds(pl.multiple_of(core * half, half), half)
    second = pl.ds(pl.multiple_of((1 - core) * half, half), half)
    experts, _, units = gate_ref.shape
    everyone = info_ref[3]
    for j in range(experts):
        mine = info_ref[2] * experts + j
        weight = jnp.sum(
            jnp.where((lane == mine) | (lane == mine + everyone), table, 0.0), axis=1, keepdims=True
        )
        gate = dot(own_all, gate_ref[j, first, :]) + dot(other_all, gate_ref[j, second, :])
        up = dot(own_all, up_ref[j, first, :]) + dot(other_all, up_ref[j, second, :])
        active = gate / (1.0 + jnp.exp(-gate)) * up
        act_ref[:, j * units : (j + 1) * units] = (active * weight).astype(bfloat16)
    total = 0.0
    for j in range(experts):
        total = total + dot(act_ref[:, j * units : (j + 1) * units], down_ref[j, :, second])
    send_ref[...] = total.astype(bfloat16)


def down_kernel(info_ref, act_ref, down_ref, keep_ref):
    half = keep_ref.shape[1]
    experts, units, _ = down_ref.shape
    first = pl.ds(pl.multiple_of(info_ref[0] * half, half), half)
    total = 0.0
    for j in range(experts):
        total = total + dot(act_ref[:, j * units : (j + 1) * units], down_ref[j, :, first])
    keep_ref[...] = total.astype(bfloat16)


def call(kernel, outs, specs, scratch=(), vmem=16, flops=0, bytes_accessed=0, **kw):
    return pl.pallas_call(
        kernel,
        out_shape=outs,
        in_specs=specs,
        out_specs=jax.tree.map(lambda _: VMEM, outs),
        scratch_shapes=scratch,
        compiler_params=pltpu.CompilerParams(vmem_limit_bytes=vmem * MIB),
        cost_estimate=pl.CostEstimate(flops=flops, bytes_accessed=bytes_accessed, transcendentals=0),
        **kw,
    )


def per_device(
    residual,
    queries,
    kv_cache,
    kv_pages,
    cache_len,
    page_row,
    page_len,
    routes,
    route_weight,
    out_weight,
    gate_weight,
    up_weight,
    down_weight,
):
    pool_size = lax.axis_size("pool")
    expert_size = lax.axis_size("expert")
    pool_index = lax.axis_index("pool")
    expert_index = lax.axis_index("expert")
    cores, near = 2, 2
    outer, far = pool_size // cores, expert_size // near
    core = pool_index % cores

    def swap(value, pool_flip=0, expert_flip=0):
        pairs = []
        for p in range(pool_size):
            for e in range(expert_size):
                pairs.append((p * expert_size + e, (p ^ pool_flip) * expert_size + (e ^ expert_flip)))
        return lax.ppermute(value, ("pool", "expert"), pairs)

    rows, steps, heads, head_dim = queries.shape
    length, kv_heads = kv_cache.shape[1:3]
    held, _, page_size = kv_pages.shape[:3]
    width = residual.shape[2]
    half = width // cores
    tokens = rows * steps
    scale = 1.0 / math.sqrt(head_dim)

    def head_of(pool):
        return pool * kv_heads // pool_size

    def pages_for(pool):
        picked = lax.dynamic_index_in_dim(kv_pages[:, 0], head_of(pool), 2, keepdims=False)
        return picked.reshape(held * page_size * 2, head_dim)

    my_head = head_of(pool_index)
    experts = gate_weight.shape[0] * expert_size
    first = (pool_index // cores == 0).astype(jnp.int32)
    whence = [pool_index ^ (k * cores) for k in range(outer)]
    whence += [p ^ 1 for p in whence]
    info = jnp.stack([core, first, expert_index, jnp.int32(experts), my_head] + whence)
    own_pages = pages_for(pool_index)
    sets = [own_pages]
    for k in range(1, outer):
        flip = k * cores
        sets.append(swap(pages_for(pool_index ^ flip), flip))
    for n in range(outer):
        sets.append(swap(sets[n], 1))

    group = steps * heads
    everything = rows * group
    q_rows = queries.reshape(everything, head_dim)
    deep = length * kv_heads * 2
    kv_rows = kv_cache.reshape(rows, deep, head_dim)
    stat = jax.ShapeDtypeStruct((everything, head_dim), float32)
    lens, owners, sizes = far_off(cache_len), far_off(page_row[:, 0]), far_off(page_len[:, 0])
    weight_half = jax.ShapeDtypeStruct((out_weight.shape[0], half), bfloat16)
    acc, top, total, weight_send, weight_keep, own_residual = call(
        functools.partial(cache_kernel, heads, kv_heads, pool_size, scale),
        (stat, stat, stat, weight_half, weight_half, jax.ShapeDtypeStruct((tokens, half), bfloat16)),
        [SMEM] * 4 + [HBM, VMEM, HBM, HBM, HBM],
        scratch=[
            pltpu.VMEM(kv_rows.shape, bfloat16),
            pltpu.VMEM(q_rows.shape, bfloat16),
            pltpu.SemaphoreType.DMA((rows,)),
            pltpu.SemaphoreType.DMA((2, 4)),
            pltpu.SemaphoreType.DMA((2,)),
        ],
        vmem=24,
        flops=4 * everything * deep * head_dim,
        bytes_accessed=kv_cache.size * 2 + out_weight.size * 2,
    )(info, lens, owners, sizes, far_off(q_rows), own_pages, far_off(kv_rows), far_off(out_weight), far_off(residual.reshape(tokens, width)))
    low, send = call(
        functools.partial(page_kernel, heads, group, pool_size, scale),
        (
            jax.ShapeDtypeStruct((tokens, heads * head_dim), bfloat16),
            jax.ShapeDtypeStruct((tokens, half), bfloat16),
        ),
        [SMEM] * 3 + [VMEM] * (4 + pool_size),
        scratch=[pltpu.VMEM((everything, head_dim), float32)] * 3,
        flops=2 * tokens * heads * head_dim * half,
    )(info, owners, sizes, q_rows, acc, top, total, *sets[1:], weight_send)
    arrived = swap(send, 1)
    keep = call(
        project_kernel, jax.ShapeDtypeStruct((tokens, half), float32), [SMEM, VMEM, VMEM, VMEM],
        flops=2 * tokens * heads * head_dim * half,
    )(info, low, weight_keep, own_residual)

    wide = -(-2 * experts // LANES) * LANES
    routes = routes.reshape(tokens, -1)
    named = routes[:, :, None] == jnp.arange(wide, dtype=jnp.int32) % experts
    table = jnp.sum(jnp.where(named, route_weight.reshape(tokens, -1, 1), 0.0), axis=1)
    coarse = lax.reduce_precision(table, 8, 7)
    table = jnp.where(jnp.arange(wide) < experts, coarse, jnp.where(jnp.arange(wide) < 2 * experts, table - coarse, 0.0))

    partial = keep + arrived.astype(float32)
    message = jnp.concatenate([partial, table], axis=1).astype(bfloat16)

    got = {(0, 0): message}
    for e in range(near):
        for k in range(outer):
            if k or e:
                got[k, e] = swap(message, k * cores, e)
    hiddens = []
    for e in range(near):
        total = got[0, e][:, :half].astype(float32)
        for k in range(1, outer):
            total = total + got[k, e][:, :half].astype(float32)
        hiddens.append(total)
    block_low = jnp.concatenate(
        [jnp.concatenate([hiddens[e].astype(bfloat16), got[0, e][:, half:]], axis=1) for e in range(near)], axis=0
    )
    gate_near, up_near, down_near = call(
        functools.partial(load_kernel, 3),
        tuple(jax.ShapeDtypeStruct(w.shape, bfloat16) for w in (gate_weight, up_weight, down_weight)),
        [ANY] + [HBM] * 3,
        scratch=[pltpu.SemaphoreType.DMA((3, 4, gate_weight.shape[0]))],
        vmem=16,
        bytes_accessed=6 * gate_weight.size,
    )(block_low, far_off(gate_weight), far_off(up_weight), far_off(down_weight))
    blocks = [block_low] + [swap(block_low, 0, k * near) for k in range(1, far)]
    others = [swap(b, 1) for b in blocks]

    everyone = tokens * near * far
    units = gate_weight.shape[0] * gate_weight.shape[2]
    act, outgoing = call(
        functools.partial(expert_kernel, far),
        (
            jax.ShapeDtypeStruct((everyone, units), bfloat16),
            jax.ShapeDtypeStruct((everyone, half), bfloat16),
        ),
        [SMEM] + [VMEM] * (2 * far + 3),
        vmem=24,
        flops=4 * everyone * width * units,
    )(info, *blocks, *others, gate_near, up_near, down_near)
    incoming = swap(outgoing, 1)
    kept = call(
        down_kernel, jax.ShapeDtypeStruct((everyone, half), bfloat16), [SMEM, VMEM, VMEM], vmem=16,
        flops=2 * everyone * half * units,
    )(info, act, down_near)
    summed = (kept.astype(float32) + incoming.astype(float32)).reshape(far, near * tokens, half)
    back = summed[0]
    for k in range(1, far):
        back = back + swap(summed[k].astype(bfloat16), 0, k * near).astype(float32)
    back = back.reshape(near, tokens, half)
    result = back[0] + hiddens[0]
    for e in range(near):
        for k in range(outer):
            if k or e:
                result = result + swap(back[e].astype(bfloat16), k * cores, e).astype(float32)
    mine = result.astype(bfloat16)
    theirs = swap(mine, 1)
    output = jnp.where(
        core == 0, jnp.concatenate([mine, theirs], axis=1), jnp.concatenate([theirs, mine], axis=1)
    )
    return output.reshape(rows, steps, width)


def solution(mesh):
    return jax.shard_map(
        per_device,
        mesh=mesh,
        in_specs=(
            P("expert", None, None),
            P("expert", None, "pool", None),
            P("expert", None, None, None, None),
            P("pool", "expert", None, None, None, None),
            P("expert"),
            P(None, "expert"),
            P(None, "expert"),
            P("expert", None, None),
            P("expert", None, None),
            P("pool", None),
            P("expert", None, "pool"),
            P("expert", None, "pool"),
            P("expert", "pool", None),
        ),
        out_specs=P("expert", None, None),
        check_vma=False,
    )
```

time: 88.3 us -> 83 us (0.940)
  local copies, waits for them, and re-layouts: 19.9 us -> 3.01 us
  Pallas kernels: 11.6 us -> 24.8 us
  waiting for transfers between devices: 35 us -> 34.1 us
    unnamed x26 -> x6, local copies, waits for them, and re-layouts: 18.4 us -> 0.01 us
    pallas_call x2 -> x3, Pallas kernels: 7.75 us -> 20.4 us  [the longest x1 10.5 us: per_device(): call(functools.partial(cache_kernel, heads, kv_heads, pool_size, scale),...]
    reshape x1, local copies, waits for them, and re-layouts: 0.05 us -> 1.61 us  [per_device(): residual.reshape(tokens, width)]
    ppermute x22, waiting for transfers between devices: 35 us -> 34.1 us  [swap(): return lax.ppermute(value, ('pool', 'expert'), pairs)]
  transfers between devices with their start and end apart: 22 -> 22, of which waited for: 16 -> 14; matrix products, arithmetic and copies ran while one was open for 2% -> 2% of each run, Pallas kernels for 8% -> 21%
where the time goes in v2:
time: 83 us; the launch traced here: 82.7 us
  waiting for transfers between devices  34.1 us (41%)
  Pallas kernels  24.8 us (30%)
  starting transfers between devices  19.3 us (23%)
  local copies, waits for them, and re-layouts  3.01 us (4%)
  other arithmetic  1.33 us (2%)
    ppermute x22, waiting for transfers between devices, swap(): return lax.ppermute(value, ('pool', 'expert'), pairs)  34.1 us
    ppermute x22, starting transfers between devices, swap(): return lax.ppermute(value, ('pool', 'expert'), pairs)  19.3 us
    pallas_call x1, Pallas kernels, per_device(): call(functools.partial(cache_kernel, heads, kv_heads, pool_size, scale),...  10.5 us
    pallas_call x1, Pallas kernels, per_device(): call(functools.partial(page_kernel, heads, group, pool_size, scale), (jax...  5.08 us
    pallas_call x1, Pallas kernels, per_device(): call(functools.partial(load_kernel, 3), tuple((jax.ShapeDtypeStruct(w.sha...  4.77 us
    pallas_call x1, Pallas kernels, per_device(): call(functools.partial(expert_kernel, far), (jax.ShapeDtypeStruct((everyo...  2.27 us
  transfers between devices with their start and end apart: 22, of which 14 were waited for; matrix products, arithmetic and copies ran while one was open for 2% of the time, Pallas kernels for 21%

profile of v2, /device:TPU:0, one launch (start us, length us, event | category | flops | bytes accessed | tf_op | source)
XLA Modules:
  0.0 82.7 jit_solution(3184755188746947424)
XLA Ops:
  0.0 1.1 %constant_dynamic-slice_fusion = (bf16[4,1,64,1,2,128]{5,4,3,2,1,0:T(2,128)(2,1)S(1)}, bf16[4,1,64,1,2,128]{5,4,3,2,1,0:T(2,128)(2,1)S(1)}) fusion(bf16[4,1,64,2,2,128]{5,4,3,2,1,0:T(2,128)(2,1)} %param.16, s32[]{:T(128)S(6)} %select_n.62, s32[]{:T(128)S(6)} %select_n.60), kind=kLoop, calls=%fused_computation.22 | loop fusion | bytes 524296 | tf_op jit(solution)/shard_map/jit(dynamic_index_in_dim)/dynamic_slice | solution.py:252
  1.2 3.1 %collective-permute-start = (bf16[512,128]{1,0:T(8,128)(2,1)S(1)}, bf16[512,128]{1,0:T(8,128)(2,1)S(1)}, u32[]{:S(2)}, u32[]{:S(2)}) collective-permute-start(bf16[512,128]{1,0:T(8,128)(2,1)S(1)} %bitcast.21), channel_id=1, source_target_pairs={{0,16},{1,17},{2,18},{3,19},{4,20},{5,21},{6,22},{7,23},{8,24},{9,... | collective-permute-start | bytes 393224 | tf_op jit(solution)/shard_map/ppermute | solution.py:238
  4.2 0.0 collective-permute-start.1
  4.2 1.6 %reshape.55.residual_hbm = bf16[16,4096]{1,0:T(8,128)(2,1)} reshape(bf16[8,2,4096]{2,1,0:T(2,128)(2,1)} %param.13) | data formatting | bytes 262144 | tf_op jit(solution)/shard_map/reshape | solution.py:291
  5.8 0.1 stack.39.info_ref
  5.9 1.8 %collective-permute-done.rest_0_ = bf16[512,128]{1,0:T(8,128)(2,1)S(1)} collective-permute-done((bf16[512,128]{1,0:T(8,128)(2,1)S(1)}, bf16[512,128]{1,0:T(8,128)(2,1)S(1)}, u32[]{:S(2)}, u32[]{:S(2)}) %collective-permute-start) | collective-permute-done | bytes 131104 | tf_op jit(solution)/shard_map/ppermute | solution.py:238
  7.7 0.0 collective-permute-start.2
  7.7 0.0 copy-start.1
  7.7 10.5 %shard_map.127 = (f32[128,128]{1,0:T(8,128)S(1)}, f32[128,128]{1,0:T(8,128)S(1)}, f32[128,128]{1,0:T(8,128)S(1)}, bf16[1024,2048]{1,0:T(8,128)(2,1)S(1)}, bf16[1...) custom-call(s32[9]{0:T(128)S(1)} %stack.39.info_ref, s32[8]{0:T(128)} %len_ref.1, s32[16]{0:T(128)} %bitcast.24, ...), custom_call_target="tpu_custom_call" | custom-call | flops 134217728 | bytes 12582912 | tf_op jit(solution)/shard_map/pallas_call | solution.py:277
  18.2 0.0 copy-done.1
  18.3 0.0 copy-done.2
  18.3 0.1 select_reduce_fusion
  18.4 0.0 collective-permute-done.1.rest_1_
  18.4 0.0 collective-permute-done.2.rest_2_
  18.4 0.0 copy-done
  18.4 5.1 %shard_map.128 = (bf16[16,1024]{1,0:T(8,128)(2,1)S(1)}, bf16[16,2048]{1,0:T(8,128)(2,1)S(1)}) custom-call(s32[9]{0:T(128)S(1)} %stack.39.info_ref, s32[16]{0:T(128)} %bitcast.25, s32[16]{0:T(128)} %bitcast.27, bf16[128,128]{1,0:T(8,128)(2,1)S(1)} %bitcast.19, f32[128,128]{1,0:T(8,128)S(1)} %get-tuple-element.18.acc_in, ...), custom_call_target="tpu_custom_call" | custom-call | flops 67108864 | tf_op jit(solution)/shard_map/pallas_call | solution.py:292
  23.5 0.4 collective-permute-start.3
  23.9 1.2 %shard_map.129 = f32[16,2048]{1,0:T(8,128)S(1)} custom-call(s32[9]{0:T(128)S(1)} %stack.39.info_ref, bf16[16,1024]{1,0:T(8,128)(2,1)S(1)} %get-tuple-element.22.low_ref, bf16[1024,2048]{1,0:T(8,128)(2,1)S(1)} %get-tuple-element.23.weight_ref, bf16[16,2048]{1,0:T(8,128)(2,1)S(1)} %get-tuple-element.24.residual_ref), custom_call_target="tpu_custom_call" | custom-call | flops 67108864 | tf_op jit(solution)/shard_map/pallas_call | solution.py:303
  25.1 0.0 collective-permute-done.3
  25.2 2.7 %collective-permute-start.6 = (bf16[16,2176]{1,0:T(8,128)(2,1)S(1)}, bf16[16,2176]{1,0:T(8,128)(2,1)S(1)}, u32[]{:S(2)}, u32[]{:S(2)}) collective-permute-start(bf16[16,2176]{1,0:T(8,128)(2,1)S(1)} %pad_maximum_fusion), channel_id=1, source_target_pairs={{0,17},{1,16},{2,19},{3,18},{4,21},{5,20},{6,23},{7,22},{8,25},{9,... | collective-permute-start | bytes 208904 | tf_op jit(solution)/shard_map/ppermute | solution.py:238
  27.9 0.5 collective-permute-start.5
  28.4 0.3 collective-permute-start.4
  28.7 1.9 %collective-permute-done.6 = bf16[16,2176]{1,0:T(8,128)(2,1)S(1)} collective-permute-done((bf16[16,2176]{1,0:T(8,128)(2,1)S(1)}, bf16[16,2176]{1,0:T(8,128)(2,1)S(1)}, u32[]{:S(2)}, u32[]{:S(2)}) %collective-permute-start.6) | collective-permute-done | bytes 69664 | tf_op jit(solution)/shard_map/ppermute | solution.py:238
  30.6 1.6 %collective-permute-done.5 = bf16[16,2176]{1,0:T(8,128)(2,1)S(1)} collective-permute-done((bf16[16,2176]{1,0:T(8,128)(2,1)S(1)}, bf16[16,2176]{1,0:T(8,128)(2,1)S(1)}, u32[]{:S(2)}, u32[]{:S(2)}) %collective-permute-start.5) | collective-permute-done | bytes 69664 | tf_op jit(solution)/shard_map/ppermute | solution.py:238
  32.3 0.5 collective-permute-done.4
  32.8 3.7 %collective-permute-start.9 = (bf16[32,2176]{1,0:T(8,128)(2,1)S(1)}, bf16[32,2176]{1,0:T(8,128)(2,1)S(1)}, u32[]{:S(2)}, u32[]{:S(2)}) collective-permute-start(bf16[32,2176]{1,0:T(8,128)(2,1)S(1)} %maximum_maximum_fusion.refs_0_.rest_0_), channel_id=1, source_target_pairs={{0,6},{1,7},{2,4},{3,5},{4,2},{5,3},{6,0},{7,1},{8,14},{9,15},{10,... | collective-permute-start | bytes 417800 | tf_op jit(solution)/shard_map/ppermute | solution.py:238
  36.5 0.0 collective-permute-start.8
  36.5 0.8 collective-permute-start.7
  37.3 0.0 collective-permute-start.10
  37.3 4.0 %collective-permute-done.9.rest_3_ = bf16[32,2176]{1,0:T(8,128)(2,1)S(1)} collective-permute-done((bf16[32,2176]{1,0:T(8,128)(2,1)S(1)}, bf16[32,2176]{1,0:T(8,128)(2,1)S(1)}, u32[]{:S(2)}, u32[]{:S(2)}) %collective-permute-start.9) | collective-permute-done | bytes 139296 | tf_op jit(solution)/shard_map/ppermute | solution.py:238
  41.2 0.0 collective-permute-start.13
  41.2 6.1 %collective-permute-done.8.rest_2_ = bf16[32,2176]{1,0:T(8,128)(2,1)S(1)} collective-permute-done((bf16[32,2176]{1,0:T(8,128)(2,1)S(1)}, bf16[32,2176]{1,0:T(8,128)(2,1)S(1)}, u32[]{:S(2)}, u32[]{:S(2)}) %collective-permute-start.8) | collective-permute-done | bytes 139296 | tf_op jit(solution)/shard_map/ppermute | solution.py:238
  47.3 0.0 collective-permute-start.12
  47.3 0.0 collective-permute-done.7.rest_1_
  47.3 0.5 collective-permute-start.11
  47.9 4.8 %shard_map.130 = (bf16[2,4096,256]{2,1,0:T(8,128)(2,1)S(1)}, bf16[2,4096,256]{2,1,0:T(8,128)(2,1)S(1)}, bf16[2,256,4096]{2,1,0:T(8,128)(2,1)S(1)}) custom-call(bf16[32,2176]{1,0:T(8,128)(2,1)S(1)} %maximum_maximum_fusion.refs_0_.rest_0_, bf16[2,4096,256]{2,1,0:T(8,128)(2,1)} %refs_1_.1, bf16[2,4096,256]{2,1,0:T(8,128)(2,1)} %refs_2_.1, ...), custom_call_target="tpu_custom_call" | custom-call | bytes 12582912 | tf_op jit(solution)/shard_map/pallas_call | solution.py:332
  52.6 0.0 collective-permute-done.10.rest_4_
  52.6 0.0 collective-permute-done.13.rest_7_
  52.7 0.0 collective-permute-done.12.rest_6_
  52.7 0.0 collective-permute-done.11.rest_5_
  52.7 2.3 %shard_map.131 = (bf16[128,512]{1,0:T(8,128)(2,1)S(1)}, bf16[128,2048]{1,0:T(8,128)(2,1)S(1)}) custom-call(s32[9]{0:T(128)S(1)} %stack.39.info_ref, bf16[32,2176]{1,0:T(8,128)(2,1)S(1)} %maximum_maximum_fusion.refs_0_.rest_0_, bf16[32,2176]{1,0:T(8,128)(2,1)S(1)} %collective-permute-done.7.rest_1_, bf16[32,2176]{1,0:T(8,128)(2,1)S(1)} %collective-permute-done.8.rest_2_, ...), custom_call_target="tpu_custom_call" | custom-call | flops 1073741824 | tf_op jit(solution)/shard_map/pallas_call | solution.py:345
  55.0 0.1 collective-permute-start.14
  55.0 1.0 %shard_map.132 = bf16[128,2048]{1,0:T(8,128)(2,1)S(1)} custom-call(s32[9]{0:T(128)S(1)} %stack.39.info_ref, bf16[128,512]{1,0:T(8,128)(2,1)S(1)} %get-tuple-element.29.act_ref, bf16[2,256,4096]{2,1,0:T(8,128)(2,1)S(1)} %get-tuple-element.28.rest_10_.down_ref), custom_call_target="tpu_custom_call" | custom-call | flops 268435456 | tf_op jit(solution)/shard_map/pallas_call | solution.py:356
  56.0 0.9 %collective-permute-done.14 = bf16[128,2048]{1,0:T(8,128)(2,1)S(1)} collective-permute-done((bf16[128,2048]{1,0:T(8,128)(2,1)S(1)}, bf16[128,2048]{1,0:T(8,128)(2,1)S(1)}, u32[]{:S(2)}, u32[]{:S(2)}) %collective-permute-start.14) | collective-permute-done | bytes 524320 | tf_op jit(solution)/shard_map/ppermute | solution.py:238
  56.9 0.2 fusion.5
  57.1 0.1 collective-permute-start.15
  57.2 2.5 %collective-permute-start.17 = (bf16[32,2048]{1,0:T(8,128)(2,1)S(1)}, bf16[32,2048]{1,0:T(8,128)(2,1)S(1)}, u32[]{:S(2)}, u32[]{:S(2)}) collective-permute-start(bf16[32,2048]{1,0:T(8,128)(2,1)S(1)} %get-tuple-element.34), channel_id=1, source_target_pairs={{0,6},{1,7},{2,4},{3,5},{4,2},{5,3},{6,0},{7,1},{8,14},{9,15},{10,... | collective-permute-start | bytes 393224 | tf_op jit(solution)/shard_map/ppermute | solution.py:238
  59.8 0.9 %collective-permute-start.16 = (bf16[32,2048]{1,0:T(8,128)(2,1)S(1)}, bf16[32,2048]{1,0:T(8,128)(2,1)S(1)}, u32[]{:S(2)}, u32[]{:S(2)}) collective-permute-start(bf16[32,2048]{1,0:T(8,128)(2,1)S(1)} %get-tuple-element.35), channel_id=1, source_target_pairs={{0,4},{1,5},{2,6},{3,7},{4,0},{5,1},{6,2},{7,3},{8,12},{9,13},{10,... | collective-permute-start | bytes 393224 | tf_op jit(solution)/shard_map/ppermute | solution.py:238
  60.7 2.0 %collective-permute-done.15 = bf16[32,2048]{1,0:T(8,128)(2,1)S(1)} collective-permute-done((bf16[32,2048]{1,0:T(8,128)(2,1)S(1)}, bf16[32,2048]{1,0:T(8,128)(2,1)S(1)}, u32[]{:S(2)}, u32[]{:S(2)}) %collective-permute-start.15) | collective-permute-done | bytes 131104 | tf_op jit(solution)/shard_map/ppermute | solution.py:238
  62.7 4.2 %collective-permute-done.17 = bf16[32,2048]{1,0:T(8,128)(2,1)S(1)} collective-permute-done((bf16[32,2048]{1,0:T(8,128)(2,1)S(1)}, bf16[32,2048]{1,0:T(8,128)(2,1)S(1)}, u32[]{:S(2)}, u32[]{:S(2)}) %collective-permute-start.17) | collective-permute-done | bytes 131104 | tf_op jit(solution)/shard_map/ppermute | solution.py:238
  66.9 5.4 %collective-permute-done.16 = bf16[32,2048]{1,0:T(8,128)(2,1)S(1)} collective-permute-done((bf16[32,2048]{1,0:T(8,128)(2,1)S(1)}, bf16[32,2048]{1,0:T(8,128)(2,1)S(1)}, u32[]{:S(2)}, u32[]{:S(2)}) %collective-permute-start.16) | collective-permute-done | bytes 131104 | tf_op jit(solution)/shard_map/ppermute | solution.py:238
  72.3 0.1 fusion.1
  72.4 1.5 %collective-permute-start.18 = (bf16[16,2048]{1,0:T(8,128)(2,1)S(1)}, bf16[16,2048]{1,0:T(8,128)(2,1)S(1)}, u32[]{:S(2)}, u32[]{:S(2)}) collective-permute-start(bf16[16,2048]{1,0:T(8,128)(2,1)S(1)} %get-tuple-element.36), channel_id=1, source_target_pairs={{0,16},{1,17},{2,18},{3,19},{4,20},{5,21},{6,22},{7,23},{8,24},{9,... | collective-permute-start | bytes 196616 | tf_op jit(solution)/shard_map/ppermute | solution.py:238
  74.0 1.3 %collective-permute-start.19 = (bf16[16,2048]{1,0:T(8,128)(2,1)S(1)}, bf16[16,2048]{1,0:T(8,128)(2,1)S(1)}, u32[]{:S(2)}, u32[]{:S(2)}) collective-permute-start(bf16[16,2048]{1,0:T(8,128)(2,1)S(1)} %get-tuple-element.37), channel_id=1, source_target_pairs={{0,1},{1,0},{2,3},{3,2},{4,5},{5,4},{6,7},{7,6},{8,9},{9,8},{10,11... | collective-permute-start | bytes 196616 | tf_op jit(solution)/shard_map/ppermute | solution.py:238
  75.3 0.7 collective-permute-start.20
  76.0 0.8 collective-permute-done.18
  76.8 1.5 %collective-permute-done.19 = bf16[16,2048]{1,0:T(8,128)(2,1)S(1)} collective-permute-done((bf16[16,2048]{1,0:T(8,128)(2,1)S(1)}, bf16[16,2048]{1,0:T(8,128)(2,1)S(1)}, u32[]{:S(2)}, u32[]{:S(2)}) %collective-permute-start.19) | collective-permute-done | bytes 65568 | tf_op jit(solution)/shard_map/ppermute | solution.py:238
  78.3 2.2 %collective-permute-done.20 = bf16[16,2048]{1,0:T(8,128)(2,1)S(1)} collective-permute-done((bf16[16,2048]{1,0:T(8,128)(2,1)S(1)}, bf16[16,2048]{1,0:T(8,128)(2,1)S(1)}, u32[]{:S(2)}, u32[]{:S(2)}) %collective-permute-start.20) | collective-permute-done | bytes 65568 | tf_op jit(solution)/shard_map/ppermute | solution.py:238
  80.5 0.1 add_convert_fusion
  80.5 0.1 collective-permute-start.21
  80.6 0.1 concatenate.29
  80.6 1.2 %collective-permute-done.21 = bf16[16,2048]{1,0:T(8,128)(2,1)S(1)} collective-permute-done((bf16[16,2048]{1,0:T(8,128)(2,1)S(1)}, bf16[16,2048]{1,0:T(8,128)(2,1)S(1)}, u32[]{:S(2)}, u32[]{:S(2)}) %collective-permute-start.21) | collective-permute-done | bytes 65568 | tf_op jit(solution)/shard_map/ppermute | solution.py:238
  81.8 0.1 concatenate.30
  81.9 0.9 %broadcast_select_fusion = bf16[8,2,4096]{2,1,0:T(2,128)(2,1)} fusion(pred[]{:T(512)S(6)} %eq.25, bf16[8,2,2048]{2,1,0:T(2,128)(2,1)S(1)} %concatenate.30, bf16[8,2,2048]{2,1,0:T(2,128)(2,1)S(1)} %concatenate.29), kind=kLoop, calls=%fused_computation.4 | loop fusion | flops 589824 | bytes 262145 | tf_op jit(solution)/shard_map/jit(_where)/select_n | solution.py:372
  (13 shorter events, 0.1 us)
Async XLA Ops:
  1.2 6.6 %collective-permute-start = (bf16[512,128]{1,0:T(8,128)(2,1)S(1)}, bf16[512,128]{1,0:T(8,128)(2,1)S(1)}, u32[]{:S(2)}, u32[]{:S(2)}) collective-permute-start(bf16[512,128]{1,0:T(8,128)(2,1)S(1)} %bitcast.21), channel_id=1, source_target_pairs={{0,16},{1,17},{2,18},{3,19},{4,20},{5,21},{6,22},{7,23},{8,24},{9,... | collective-permute-start | bytes 393224 | tf_op jit(solution)/shard_map/ppermute | solution.py:238
  4.2 14.2 %collective-permute-start.1 = (bf16[512,128]{1,0:T(8,128)(2,1)S(1)}, bf16[512,128]{1,0:T(8,128)(2,1)S(1)}, u32[]{:S(2)}, u32[]{:S(2)}) collective-permute-start(bf16[512,128]{1,0:T(8,128)(2,1)S(1)} %bitcast.16), channel_id=1, source_target_pairs={{0,8},{1,9},{2,10},{3,11},{4,12},{5,13},{6,14},{7,15},{8,0},{9,1},... | collective-permute-start | bytes 393224 | tf_op jit(solution)/shard_map/ppermute | solution.py:238
  7.7 10.7 %collective-permute-start.2 = (bf16[512,128]{1,0:T(8,128)(2,1)S(1)}, bf16[512,128]{1,0:T(8,128)(2,1)S(1)}, u32[]{:S(2)}, u32[]{:S(2)}) collective-permute-start(bf16[512,128]{1,0:T(8,128)(2,1)S(1)} %collective-permute-done.rest_0_), channel_id=1, source_target_pairs={{0,8},{1,9},{2,10},{3,11},{4,12},{5,13},{6,14},{7,15},{8,0},{9,1},... | collective-permute-start | bytes 393224 | tf_op jit(solution)/shard_map/ppermute | solution.py:238
  7.7 10.5 %copy-start.1 = (f32[8,2,8]{2,1,0:T(2,128)S(1)}, f32[8,2,8]{2,1,0:T(2,128)}, u32[]{:S(2)}) copy-start(f32[8,2,8]{2,1,0:T(2,128)} %param.21) | copy-start | bytes 1540
  7.7 10.5 %copy-start.2 = (s32[8,2,8]{2,1,0:T(2,128)S(1)}, s32[8,2,8]{2,1,0:T(2,128)}, u32[]{:S(2)}) copy-start(s32[8,2,8]{2,1,0:T(2,128)} %param.20) | copy-start | bytes 1540
  7.7 10.7 %copy-start = (bf16[8,2,8,128]{3,2,1,0:T(8,128)(2,1)S(1)}, bf16[8,2,8,128]{3,2,1,0:T(8,128)(2,1)}, u32[]{:S(2)}) copy-start(bf16[8,2,8,128]{3,2,1,0:T(8,128)(2,1)} %param.14) | copy-start | bytes 98308
  23.5 1.6 %collective-permute-start.3 = (bf16[16,2048]{1,0:T(8,128)(2,1)S(1)}, bf16[16,2048]{1,0:T(8,128)(2,1)S(1)}, u32[]{:S(2)}, u32[]{:S(2)}) collective-permute-start(bf16[16,2048]{1,0:T(8,128)(2,1)S(1)} %get-tuple-element.25), channel_id=1, source_target_pairs={{0,8},{1,9},{2,10},{3,11},{4,12},{5,13},{6,14},{7,15},{8,0},{9,1},... | collective-permute-start | bytes 196616 | tf_op jit(solution)/shard_map/ppermute | solution.py:238
  25.2 5.5 %collective-permute-start.6 = (bf16[16,2176]{1,0:T(8,128)(2,1)S(1)}, bf16[16,2176]{1,0:T(8,128)(2,1)S(1)}, u32[]{:S(2)}, u32[]{:S(2)}) collective-permute-start(bf16[16,2176]{1,0:T(8,128)(2,1)S(1)} %pad_maximum_fusion), channel_id=1, source_target_pairs={{0,17},{1,16},{2,19},{3,18},{4,21},{5,20},{6,23},{7,22},{8,25},{9,... | collective-permute-start | bytes 208904 | tf_op jit(solution)/shard_map/ppermute | solution.py:238
  27.9 4.3 %collective-permute-start.5 = (bf16[16,2176]{1,0:T(8,128)(2,1)S(1)}, bf16[16,2176]{1,0:T(8,128)(2,1)S(1)}, u32[]{:S(2)}, u32[]{:S(2)}) collective-permute-start(bf16[16,2176]{1,0:T(8,128)(2,1)S(1)} %pad_maximum_fusion), channel_id=1, source_target_pairs={{0,1},{1,0},{2,3},{3,2},{4,5},{5,4},{6,7},{7,6},{8,9},{9,8},{10,11... | collective-permute-start | bytes 208904 | tf_op jit(solution)/shard_map/ppermute | solution.py:238
  28.4 4.3 %collective-permute-start.4 = (bf16[16,2176]{1,0:T(8,128)(2,1)S(1)}, bf16[16,2176]{1,0:T(8,128)(2,1)S(1)}, u32[]{:S(2)}, u32[]{:S(2)}) collective-permute-start(bf16[16,2176]{1,0:T(8,128)(2,1)S(1)} %pad_maximum_fusion), channel_id=1, source_target_pairs={{0,16},{1,17},{2,18},{3,19},{4,20},{5,21},{6,22},{7,23},{8,24},{9,... | collective-permute-start | bytes 208904 | tf_op jit(solution)/shard_map/ppermute | solution.py:238
  32.8 8.4 %collective-permute-start.9 = (bf16[32,2176]{1,0:T(8,128)(2,1)S(1)}, bf16[32,2176]{1,0:T(8,128)(2,1)S(1)}, u32[]{:S(2)}, u32[]{:S(2)}) collective-permute-start(bf16[32,2176]{1,0:T(8,128)(2,1)S(1)} %maximum_maximum_fusion.refs_0_.rest_0_), channel_id=1, source_target_pairs={{0,6},{1,7},{2,4},{3,5},{4,2},{5,3},{6,0},{7,1},{8,14},{9,15},{10,... | collective-permute-start | bytes 417800 | tf_op jit(solution)/shard_map/ppermute | solution.py:238
  36.5 10.9 %collective-permute-start.8 = (bf16[32,2176]{1,0:T(8,128)(2,1)S(1)}, bf16[32,2176]{1,0:T(8,128)(2,1)S(1)}, u32[]{:S(2)}, u32[]{:S(2)}) collective-permute-start(bf16[32,2176]{1,0:T(8,128)(2,1)S(1)} %maximum_maximum_fusion.refs_0_.rest_0_), channel_id=1, source_target_pairs={{0,4},{1,5},{2,6},{3,7},{4,0},{5,1},{6,2},{7,3},{8,12},{9,13},{10,... | collective-permute-start | bytes 417800 | tf_op jit(solution)/shard_map/ppermute | solution.py:238
  36.5 10.9 %collective-permute-start.7 = (bf16[32,2176]{1,0:T(8,128)(2,1)S(1)}, bf16[32,2176]{1,0:T(8,128)(2,1)S(1)}, u32[]{:S(2)}, u32[]{:S(2)}) collective-permute-start(bf16[32,2176]{1,0:T(8,128)(2,1)S(1)} %maximum_maximum_fusion.refs_0_.rest_0_), channel_id=1, source_target_pairs={{0,2},{1,3},{2,0},{3,1},{4,6},{5,7},{6,4},{7,5},{8,10},{9,11},{10,... | collective-permute-start | bytes 417800 | tf_op jit(solution)/shard_map/ppermute | solution.py:238
  37.3 15.4 %collective-permute-start.10 = (bf16[32,2176]{1,0:T(8,128)(2,1)S(1)}, bf16[32,2176]{1,0:T(8,128)(2,1)S(1)}, u32[]{:S(2)}, u32[]{:S(2)}) collective-permute-start(bf16[32,2176]{1,0:T(8,128)(2,1)S(1)} %maximum_maximum_fusion.refs_0_.rest_0_), channel_id=1, source_target_pairs={{0,8},{1,9},{2,10},{3,11},{4,12},{5,13},{6,14},{7,15},{8,0},{9,1},... | collective-permute-start | bytes 417800 | tf_op jit(solution)/shard_map/ppermute | solution.py:238
  41.2 11.4 %collective-permute-start.13 = (bf16[32,2176]{1,0:T(8,128)(2,1)S(1)}, bf16[32,2176]{1,0:T(8,128)(2,1)S(1)}, u32[]{:S(2)}, u32[]{:S(2)}) collective-permute-start(bf16[32,2176]{1,0:T(8,128)(2,1)S(1)} %collective-permute-done.9.rest_3_), channel_id=1, source_target_pairs={{0,8},{1,9},{2,10},{3,11},{4,12},{5,13},{6,14},{7,15},{8,0},{9,1},... | collective-permute-start | bytes 417800 | tf_op jit(solution)/shard_map/ppermute | solution.py:238
  47.3 5.3 %collective-permute-start.12 = (bf16[32,2176]{1,0:T(8,128)(2,1)S(1)}, bf16[32,2176]{1,0:T(8,128)(2,1)S(1)}, u32[]{:S(2)}, u32[]{:S(2)}) collective-permute-start(bf16[32,2176]{1,0:T(8,128)(2,1)S(1)} %collective-permute-done.8.rest_2_), channel_id=1, source_target_pairs={{0,8},{1,9},{2,10},{3,11},{4,12},{5,13},{6,14},{7,15},{8,0},{9,1},... | collective-permute-start | bytes 417800 | tf_op jit(solution)/shard_map/ppermute | solution.py:238
  47.3 5.3 %collective-permute-start.11 = (bf16[32,2176]{1,0:T(8,128)(2,1)S(1)}, bf16[32,2176]{1,0:T(8,128)(2,1)S(1)}, u32[]{:S(2)}, u32[]{:S(2)}) collective-permute-start(bf16[32,2176]{1,0:T(8,128)(2,1)S(1)} %collective-permute-done.7.rest_1_), channel_id=1, source_target_pairs={{0,8},{1,9},{2,10},{3,11},{4,12},{5,13},{6,14},{7,15},{8,0},{9,1},... | collective-permute-start | bytes 417800 | tf_op jit(solution)/shard_map/ppermute | solution.py:238
  55.0 2.0 %collective-permute-start.14 = (bf16[128,2048]{1,0:T(8,128)(2,1)S(1)}, bf16[128,2048]{1,0:T(8,128)(2,1)S(1)}, u32[]{:S(2)}, u32[]{:S(2)}) collective-permute-start(bf16[128,2048]{1,0:T(8,128)(2,1)S(1)} %get-tuple-element.30), channel_id=1, source_target_pairs={{0,8},{1,9},{2,10},{3,11},{4,12},{5,13},{6,14},{7,15},{8,0},{9,1},... | collective-permute-start | bytes 1572872 | tf_op jit(solution)/shard_map/ppermute | solution.py:238
  57.1 5.6 %collective-permute-start.15 = (bf16[32,2048]{1,0:T(8,128)(2,1)S(1)}, bf16[32,2048]{1,0:T(8,128)(2,1)S(1)}, u32[]{:S(2)}, u32[]{:S(2)}) collective-permute-start(bf16[32,2048]{1,0:T(8,128)(2,1)S(1)} %get-tuple-element.33), channel_id=1, source_target_pairs={{0,2},{1,3},{2,0},{3,1},{4,6},{5,7},{6,4},{7,5},{8,10},{9,11},{10,... | collective-permute-start | bytes 393224 | tf_op jit(solution)/shard_map/ppermute | solution.py:238
  57.2 9.7 %collective-permute-start.17 = (bf16[32,2048]{1,0:T(8,128)(2,1)S(1)}, bf16[32,2048]{1,0:T(8,128)(2,1)S(1)}, u32[]{:S(2)}, u32[]{:S(2)}) collective-permute-start(bf16[32,2048]{1,0:T(8,128)(2,1)S(1)} %get-tuple-element.34), channel_id=1, source_target_pairs={{0,6},{1,7},{2,4},{3,5},{4,2},{5,3},{6,0},{7,1},{8,14},{9,15},{10,... | collective-permute-start | bytes 393224 | tf_op jit(solution)/shard_map/ppermute | solution.py:238
  59.8 12.6 %collective-permute-start.16 = (bf16[32,2048]{1,0:T(8,128)(2,1)S(1)}, bf16[32,2048]{1,0:T(8,128)(2,1)S(1)}, u32[]{:S(2)}, u32[]{:S(2)}) collective-permute-start(bf16[32,2048]{1,0:T(8,128)(2,1)S(1)} %get-tuple-element.35), channel_id=1, source_target_pairs={{0,4},{1,5},{2,6},{3,7},{4,0},{5,1},{6,2},{7,3},{8,12},{9,13},{10,... | collective-permute-start | bytes 393224 | tf_op jit(solution)/shard_map/ppermute | solution.py:238
  72.4 4.3 %collective-permute-start.18 = (bf16[16,2048]{1,0:T(8,128)(2,1)S(1)}, bf16[16,2048]{1,0:T(8,128)(2,1)S(1)}, u32[]{:S(2)}, u32[]{:S(2)}) collective-permute-start(bf16[16,2048]{1,0:T(8,128)(2,1)S(1)} %get-tuple-element.36), channel_id=1, source_target_pairs={{0,16},{1,17},{2,18},{3,19},{4,20},{5,21},{6,22},{7,23},{8,24},{9,... | collective-permute-start | bytes 196616 | tf_op jit(solution)/shard_map/ppermute | solution.py:238
  74.0 4.3 %collective-permute-start.19 = (bf16[16,2048]{1,0:T(8,128)(2,1)S(1)}, bf16[16,2048]{1,0:T(8,128)(2,1)S(1)}, u32[]{:S(2)}, u32[]{:S(2)}) collective-permute-start(bf16[16,2048]{1,0:T(8,128)(2,1)S(1)} %get-tuple-element.37), channel_id=1, source_target_pairs={{0,1},{1,0},{2,3},{3,2},{4,5},{5,4},{6,7},{7,6},{8,9},{9,8},{10,11... | collective-permute-start | bytes 196616 | tf_op jit(solution)/shard_map/ppermute | solution.py:238
  75.3 5.2 %collective-permute-start.20 = (bf16[16,2048]{1,0:T(8,128)(2,1)S(1)}, bf16[16,2048]{1,0:T(8,128)(2,1)S(1)}, u32[]{:S(2)}, u32[]{:S(2)}) collective-permute-start(bf16[16,2048]{1,0:T(8,128)(2,1)S(1)} %get-tuple-element.37), channel_id=1, source_target_pairs={{0,17},{1,16},{2,19},{3,18},{4,21},{5,20},{6,23},{7,22},{8,25},{9,... | collective-permute-start | bytes 196616 | tf_op jit(solution)/shard_map/ppermute | solution.py:238
  80.5 1.3 %collective-permute-start.21 = (bf16[16,2048]{1,0:T(8,128)(2,1)S(1)}, bf16[16,2048]{1,0:T(8,128)(2,1)S(1)}, u32[]{:S(2)}, u32[]{:S(2)}) collective-permute-start(bf16[16,2048]{1,0:T(8,128)(2,1)S(1)} %add_convert_fusion), channel_id=1, source_target_pairs={{0,8},{1,9},{2,10},{3,11},{4,12},{5,13},{6,14},{7,15},{8,0},{9,1},... | collective-permute-start | bytes 196616 | tf_op jit(solution)/shard_map/ppermute | solution.py:238
